TPU v7x, 256 devices: a whole 4x4x8 slice. The times are simulated.
256 devices in a mesh: row: 8 (over y, core), col: 32 (over z, x).
Axes of the slice: x: 4, y: 4, z: 8, core: 2. Of those that a mesh axis runs over, the one named last changes fastest.
Arguments:
- right_sides: bfloat16 [1024, 64, 256], P('col', 'row'), may hold values from -6 to 6
- prior_left: bfloat16 [64, 128, 48, 1024], P('row', 'col'), may hold values from -0.15625 to 0.15625
- prior_right: bfloat16 [64, 128, 48, 1024], P('row', 'col'), may hold values from -0.1875 to 0.1875
- solved_prior: bfloat16 [128, 1024, 256], P('col', 'row'), may hold values from -6 to 6
- diag_left: bfloat16 [64, 4, 48, 1024], P('row', None, None, 'col'), may hold values from -0.4375 to 0.4375
- diag_right: bfloat16 [64, 4, 48, 1024], P('row', None, None, 'col'), may hold values from -0.1875 to 0.1875
- diag_inverse: bfloat16 [4, 1024, 1024], P(None, 'col'), may hold values from -1 to 2, as said below
Outputs:
- updated: float32 [1024, 64, 256], P('col', 'row')
- solved: bfloat16 [4, 1024, 256], P(None, 'col')
Inputs may be any that keep to these rules, and one draw needn't show every extreme that they name: `diag_inverse`: each tile is lower triangular.
All inputs are finite; a program needn't handle non-finite values.
Results may differ from a plain program's by a relative error of at most 0.012.
Values may be sent and summed in bfloat16 or wider, within the bound.
A program may use at most 64 MiB of HBM per device.

v0:
```python
import jax
import jax.numpy as jnp
from jax import lax
from jax.sharding import Mesh
from jax.sharding import PartitionSpec as P

ROW = ("row_0", "row_1")
COL = ("col_0", "col_1")


def copy_for_each(value, axis):
    count = lax.axis_size(axis)
    return lax.all_to_all(
        jnp.broadcast_to(value[None], (count, *value.shape)), axis, 0, 0, tiled=True
    )


def laid_out(blocks, dim):
    lengths = list(blocks.shape[1:])
    lengths[dim] *= blocks.shape[0]
    return jnp.moveaxis(blocks, 0, dim).reshape(lengths)


def whole_of(value, axes, dim):
    far, near = axes
    initial = copy_for_each(value, far)
    blocks = jnp.swapaxes(copy_for_each(initial, near), 0, 1)
    return laid_out(blocks.reshape(-1, *value.shape), dim)


def collect(value, axis, dim):
    return laid_out(copy_for_each(value, axis), dim)


def picked(value, axis, root):
    return lax.dynamic_index_in_dim(lax.all_gather(value, axis), root, 0, keepdims=False)


def cut_along(value, dim, count):
    before, after = (value.shape[:dim], value.shape[dim + 1 :])
    return jnp.moveaxis(value.reshape(*before, count, -1, *after), dim, 0)


def summed_on_arrival(value, axis, dim):
    count = lax.axis_size(axis)
    blocks = lax.all_to_all(cut_along(value, dim, count), axis, 0, 0, tiled=True)
    return jnp.sum(blocks, axis=0)


def padded_to(lines, count):
    spare = -len(lines) % count
    return jnp.pad(lines, [(0, spare)] + [(0, 0)] * (lines.ndim - 1))


def sum_by_parts(value, axes):
    lines = value.reshape(-1, value.shape[-1])
    own = summed_on_arrival(padded_to(lines, lax.axis_size(axes)), axes, 0)
    whole = collect(own, axes, 0)
    return whole[: len(lines)].reshape(value.shape)


def own_rows(terms, axes):
    so_far = terms.astype(jnp.bfloat16)
    for axis in axes:
        so_far = lax.psum_scatter(so_far, axis, scatter_dimension=0, tiled=True)
    return so_far.astype(jnp.float32)


def prior_term(left_block, coeff_block):
    return jnp.einsum("aprt,aprh->tah", left_block, coeff_block, preferred_element_type=jnp.float32)


def local(right_sides, prior_left, prior_right, solved_prior, diag_left, diag_right, diag_inverse):
    slice_rows = right_sides.shape[0]
    local_rows = right_sides.shape[1]
    sides_count = right_sides.shape[2]
    steps_count = diag_left.shape[1]
    row_index = lax.axis_index(ROW)
    coeff = jnp.einsum(
        "aprt,pth->aprh",
        prior_right,
        whole_of(solved_prior, ("row_0", "row_1"), 1),
        preferred_element_type=jnp.float32,
    ).astype(jnp.bfloat16)
    base = right_sides.astype(jnp.float32)
    lead_prior = summed_on_arrival(prior_term(prior_left[0:1], coeff[0:1]), COL, 0)
    leading = base[:, 0] - lead_prior[:, 0]
    solved_list = []
    trailing = jnp.zeros((slice_rows, local_rows - 1, sides_count), jnp.float32)
    for step in range(steps_count):
        block = diag_inverse[step]
        answer = jnp.dot(
            block, collect(leading.astype(jnp.bfloat16), COL, 0), preferred_element_type=jnp.float32
        ).astype(jnp.bfloat16)
        answer = picked(answer, ROW, step)
        solved_list.append(answer)
        all_terms = jnp.einsum(
            "art,th->arh", diag_right[:, step], answer, preferred_element_type=jnp.float32
        )
        all_coeff = sum_by_parts(all_terms, COL).astype(jnp.bfloat16)
        first_coeff = all_coeff[0]
        trailing = trailing + jnp.einsum(
            "art,arh->tah", diag_left[1:, step], all_coeff[1:], preferred_element_type=jnp.float32
        )
        gate = (row_index > step).astype(jnp.float32)
        leading = leading - gate * jnp.einsum(
            "rt,rh->th", diag_left[0, step], first_coeff, preferred_element_type=jnp.float32
        )
    leading, trailing, solved = (leading, trailing, jnp.stack(solved_list, 0))
    rest_prior = own_rows(prior_term(prior_left[1:], coeff[1:]), COL)
    others = base[:, 1:] - rest_prior - trailing
    updated = jnp.concatenate([leading[:, None, :], others], axis=1)
    return (updated, solved)


def solution(mesh):
    split = Mesh(mesh.devices.reshape(4, 2, 8, 4), ("row_0", "row_1", "col_0", "col_1"))
    return jax.shard_map(
        local,
        mesh=split,
        in_specs=(
            P(COL, ROW, None),
            P(ROW, COL, None, None),
            P(ROW, COL, None, None),
            P(COL, ROW, None),
            P(ROW, None, None, COL),
            P(ROW, None, None, COL),
            P(None, COL, None),
        ),
        out_specs=(P(COL, ROW, None), P(None, COL, None)),
        check_vma=False,
    )
```

profile of v0, /device:TPU:8, one launch (start us, length us, event | category | flops | bytes accessed | tf_op | source)
XLA Modules:
  0.0 426.6 jit_solution(9107070441655893991)
XLA Ops:
  8.4 18.3 %all_to_all.75 = bf16[4,4,128,256]{3,2,1,0:T(8,128)(2,1)S(1)} all-to-all(bf16[4,4,128,256]{3,2,1,0:T(8,128)(2,1)S(1)} %broadcast_in_dim.22), channel_id=1, replica_groups=mesh['row_0'=4,'row_1'=2,'col_0'=8,'col_1'=4] {'row_0'}, dimensions={0} | all-to-all | bytes 2097152 | tf_op jit(solution)/shard_map/all_to_all | solution.py:13
  27.0 5.4 %all_to_all.76 = bf16[2,4,4,128,256]{4,3,1,2,0:T(8,128)(2,1)S(1)} all-to-all(bf16[2,4,4,128,256]{4,3,1,2,0:T(8,128)(2,1)S(1)} %broadcast_in_dim.23), channel_id=1, replica_groups=mesh['row_0'=4,'row_1'=2,'col_0'=8,'col_1'=4] {'row_1'}, dimensions={0} | all-to-all | bytes 4194304 | tf_op jit(solution)/shard_map/all_to_all | solution.py:13
  34.8 2.3 convolution_bitcast_fusion
  37.2 2.5 copy.57
  39.7 11.4 %all-to-all-start.2 = ((f32[32,32,1,256]{3,1,2,0:T(8,128)}), f32[32,32,1,256]{3,1,2,0:T(8,128)}, u32[]{:S(2)}, u32[]{:S(2)}) async-start(f32[32,32,1,256]{3,1,2,0:T(8,128)} %bitcast.189), calls=%async_computation.2 | async-start | bytes 2097152 | tf_op jit(solution)/shard_map/all_to_all | solution.py:46
  51.2 28.3 %all-to-all-done.2 = f32[32,32,1,256]{3,1,2,0:T(8,128)} async-done(((f32[32,32,1,256]{3,1,2,0:T(8,128)}), f32[32,32,1,256]{3,1,2,0:T(8,128)}, u32[]{:S(2)}, u32[]{:S(2)}) %all-to-all-start.2) | async-done | bytes 1048608 | tf_op jit(solution)/shard_map/all_to_all | solution.py:46
  80.9 22.5 %all_to_all.77 = bf16[32,32,256]{2,1,0:T(8,128)(2,1)S(1)} all-to-all(bf16[32,32,256]{2,1,0:T(8,128)(2,1)S(1)} %broadcast_in_dim.24), channel_id=1, replica_groups=mesh['row_0'=4,'row_1'=2,'col_0'=8,'col_1'=4] {'col_0','col_1'}, dimensions={0} | all-to-all | bytes 1048576 | tf_op jit(solution)/shard_map/all_to_all | solution.py:13
  104.4 12.1 %all-gather = bf16[256,256]{1,0:T(8,128)(2,1)S(1)} all-gather(bf16[32,256]{1,0:T(8,128)(2,1)S(1)} %fusion.21), channel_id=2, replica_groups=mesh['row_0'=4,'row_1'=2,'col_0'=8,'col_1'=4] {'row_0','row_1'}, dimensions={0}, use_global_device_ids=true | all-gather | bytes 147456 | tf_op jit(solution)/shard_map/all_gather | solution.py:36
  119.1 23.2 %all_to_all.78 = f32[32,12,256]{2,1,0:T(8,128)} all-to-all(f32[32,12,256]{2,1,0:T(8,128)} %reshape.94), channel_id=1, replica_groups=mesh['row_0'=4,'row_1'=2,'col_0'=8,'col_1'=4] {'col_0','col_1'}, dimensions={0} | all-to-all | bytes 786432 | tf_op jit(solution)/shard_map/all_to_all | solution.py:46
  144.1 4.6 %all-to-all-start.5 = ((bf16[32,12,256]{2,1,0:T(8,128)(2,1)}), bf16[32,12,256]{2,1,0:T(8,128)(2,1)S(1)}, u32[]{:S(2)}, u32[]{:S(2)}) async-start(bf16[32,12,256]{2,1,0:T(8,128)(2,1)} %broadcast_in_dim.25), calls=%async_computation.5 | async-start | bytes 524288 | tf_op jit(solution)/shard_map/all_to_all | solution.py:13
  148.7 12.4 %all-to-all-done.5 = bf16[32,12,256]{2,1,0:T(8,128)(2,1)S(1)} async-done(((bf16[32,12,256]{2,1,0:T(8,128)(2,1)}), bf16[32,12,256]{2,1,0:T(8,128)(2,1)S(1)}, u32[]{:S(2)}, u32[]{:S(2)}) %all-to-all-start.5) | async-done | bytes 196640 | tf_op jit(solution)/shard_map/all_to_all | solution.py:13
  163.6 4.6 %all-to-all-start.6 = ((bf16[32,32,256]{2,1,0:T(8,128)(2,1)}), bf16[32,32,256]{2,1,0:T(8,128)(2,1)}, u32[]{:S(2)}, u32[]{:S(2)}) async-start(bf16[32,32,256]{2,1,0:T(8,128)(2,1)} %broadcast_in_dim.26), calls=%async_computation.6 | async-start | bytes 1048576 | tf_op jit(solution)/shard_map/all_to_all | solution.py:13
  168.3 7.8 %fusion = bf16[1024,7,256]{2,0,1:T(8,128)(2,1)} fusion(bf16[8,4,48,256]{3,2,0,1:T(8,128)(2,1)} %copy-done.12, bf16[8,4,48,1024]{3,2,1,0:T(8,128)(2,1)} %param.8), kind=kOutput, calls=%fused_computation.1 | convolution fusion | flops 706478080 | bytes 7208960 | tf_op jit(solution)/shard_map/aprt,aprh->tah/dot_general | solution.py:70
  176.1 8.4 %all-to-all-done.6 = bf16[32,32,256]{2,1,0:T(8,128)(2,1)} async-done(((bf16[32,32,256]{2,1,0:T(8,128)(2,1)}), bf16[32,32,256]{2,1,0:T(8,128)(2,1)}, u32[]{:S(2)}, u32[]{:S(2)}) %all-to-all-start.6) | async-done | bytes 524320 | tf_op jit(solution)/shard_map/all_to_all | solution.py:13
  185.8 12.7 %all-gather.1 = bf16[256,256]{1,0:T(8,128)(2,1)S(1)} all-gather(bf16[32,256]{1,0:T(8,128)(2,1)S(1)} %fusion.22), channel_id=3, replica_groups=mesh['row_0'=4,'row_1'=2,'col_0'=8,'col_1'=4] {'row_0','row_1'}, dimensions={0}, use_global_device_ids=true | all-gather | bytes 147456 | tf_op jit(solution)/shard_map/all_gather | solution.py:36
  201.1 28.5 %all_to_all.79 = f32[32,12,256]{2,1,0:T(8,128)} all-to-all(f32[32,12,256]{2,1,0:T(8,128)} %reshape.96), channel_id=1, replica_groups=mesh['row_0'=4,'row_1'=2,'col_0'=8,'col_1'=4] {'col_0','col_1'}, dimensions={0} | all-to-all | bytes 786432 | tf_op jit(solution)/shard_map/all_to_all | solution.py:46
  231.4 4.8 %all-to-all-start.8 = ((bf16[32,12,256]{2,1,0:T(8,128)(2,1)}), bf16[32,12,256]{2,1,0:T(8,128)(2,1)S(1)}, u32[]{:S(2)}, u32[]{:S(2)}) async-start(bf16[32,12,256]{2,1,0:T(8,128)(2,1)} %broadcast_in_dim.27), calls=%async_computation.8 | async-start | bytes 524288 | tf_op jit(solution)/shard_map/all_to_all | solution.py:13
  236.2 12.6 %all-to-all-done.8 = bf16[32,12,256]{2,1,0:T(8,128)(2,1)S(1)} async-done(((bf16[32,12,256]{2,1,0:T(8,128)(2,1)}), bf16[32,12,256]{2,1,0:T(8,128)(2,1)S(1)}, u32[]{:S(2)}, u32[]{:S(2)}) %all-to-all-start.8) | async-done | bytes 196640 | tf_op jit(solution)/shard_map/all_to_all | solution.py:13
  250.5 20.9 %all_to_all.80 = bf16[32,32,256]{2,1,0:T(8,128)(2,1)S(1)} all-to-all(bf16[32,32,256]{2,1,0:T(8,128)(2,1)S(1)} %broadcast_in_dim.28), channel_id=1, replica_groups=mesh['row_0'=4,'row_1'=2,'col_0'=8,'col_1'=4] {'col_0','col_1'}, dimensions={0} | all-to-all | bytes 1048576 | tf_op jit(solution)/shard_map/all_to_all | solution.py:13
  272.4 12.7 %all-gather.2 = bf16[256,256]{1,0:T(8,128)(2,1)S(1)} all-gather(bf16[32,256]{1,0:T(8,128)(2,1)S(1)} %fusion.23), channel_id=4, replica_groups=mesh['row_0'=4,'row_1'=2,'col_0'=8,'col_1'=4] {'row_0','row_1'}, dimensions={0}, use_global_device_ids=true | all-gather | bytes 147456 | tf_op jit(solution)/shard_map/all_gather | solution.py:36
  287.7 23.3 %all_to_all.81 = f32[32,12,256]{2,1,0:T(8,128)} all-to-all(f32[32,12,256]{2,1,0:T(8,128)} %reshape.98), channel_id=1, replica_groups=mesh['row_0'=4,'row_1'=2,'col_0'=8,'col_1'=4] {'col_0','col_1'}, dimensions={0} | all-to-all | bytes 786432 | tf_op jit(solution)/shard_map/all_to_all | solution.py:46
  312.8 4.7 %all-to-all-start.11 = ((bf16[32,12,256]{2,1,0:T(8,128)(2,1)}), bf16[32,12,256]{2,1,0:T(8,128)(2,1)}, u32[]{:S(2)}, u32[]{:S(2)}) async-start(bf16[32,12,256]{2,1,0:T(8,128)(2,1)} %broadcast_in_dim.29), calls=%async_computation.11 | async-start | bytes 524288 | tf_op jit(solution)/shard_map/all_to_all | solution.py:13
  317.5 12.4 %all-to-all-done.11 = bf16[32,12,256]{2,1,0:T(8,128)(2,1)} async-done(((bf16[32,12,256]{2,1,0:T(8,128)(2,1)}), bf16[32,12,256]{2,1,0:T(8,128)(2,1)}, u32[]{:S(2)}, u32[]{:S(2)}) %all-to-all-start.11) | async-done | bytes 196640 | tf_op jit(solution)/shard_map/all_to_all | solution.py:13
  333.0 4.6 %all-to-all-start.12 = ((bf16[32,32,256]{2,1,0:T(8,128)(2,1)}), bf16[32,32,256]{2,1,0:T(8,128)(2,1)}, u32[]{:S(2)}, u32[]{:S(2)}) async-start(bf16[32,32,256]{2,1,0:T(8,128)(2,1)} %broadcast_in_dim.30), calls=%async_computation.12 | async-start | bytes 1048576 | tf_op jit(solution)/shard_map/all_to_all | solution.py:13
  339.1 14.8 %all-to-all-done.12 = bf16[32,32,256]{2,1,0:T(8,128)(2,1)} async-done(((bf16[32,32,256]{2,1,0:T(8,128)(2,1)}), bf16[32,32,256]{2,1,0:T(8,128)(2,1)}, u32[]{:S(2)}, u32[]{:S(2)}) %all-to-all-start.12) | async-done | bytes 524320 | tf_op jit(solution)/shard_map/all_to_all | solution.py:13
  355.2 12.7 %all-gather.3 = bf16[256,256]{1,0:T(8,128)(2,1)S(1)} all-gather(bf16[32,256]{1,0:T(8,128)(2,1)S(1)} %fusion.24), channel_id=5, replica_groups=mesh['row_0'=4,'row_1'=2,'col_0'=8,'col_1'=4] {'row_0','row_1'}, dimensions={0}, use_global_device_ids=true | all-gather | bytes 147456 | tf_op jit(solution)/shard_map/all_gather | solution.py:36
  370.6 4.6 %all-to-all-start.13 = ((f32[32,12,256]{2,1,0:T(8,128)}), f32[32,12,256]{2,1,0:T(8,128)}, u32[]{:S(2)}, u32[]{:S(2)}) async-start(f32[32,12,256]{2,1,0:T(8,128)} %reshape.100), calls=%async_computation.13 | async-start | bytes 1048576 | tf_op jit(solution)/shard_map/all_to_all | solution.py:46
  381.1 1.9 convolution_add_fusion.2
  387.1 6.6 %all-to-all-done.13 = f32[32,12,256]{2,1,0:T(8,128)} async-done(((f32[32,12,256]{2,1,0:T(8,128)}), f32[32,12,256]{2,1,0:T(8,128)}, u32[]{:S(2)}, u32[]{:S(2)}) %all-to-all-start.13) | async-done | bytes 393248 | tf_op jit(solution)/shard_map/all_to_all | solution.py:46
  395.4 4.8 %all-to-all-start.14 = ((bf16[32,12,256]{2,1,0:T(8,128)(2,1)}), bf16[32,12,256]{2,1,0:T(8,128)(2,1)}, u32[]{:S(2)}, u32[]{:S(2)}) async-start(bf16[32,12,256]{2,1,0:T(8,128)(2,1)} %broadcast_in_dim.31), calls=%async_computation.14 | async-start | bytes 524288 | tf_op jit(solution)/shard_map/all_to_all | solution.py:13
  400.3 1.9 convolution_add_fusion.1
  403.6 9.1 %all-to-all-done.14 = bf16[32,12,256]{2,1,0:T(8,128)(2,1)} async-done(((bf16[32,12,256]{2,1,0:T(8,128)(2,1)}), bf16[32,12,256]{2,1,0:T(8,128)(2,1)}, u32[]{:S(2)}, u32[]{:S(2)}) %all-to-all-start.14) | async-done | bytes 196640 | tf_op jit(solution)/shard_map/all_to_all | solution.py:13
  (95 shorter events, 54.6 us)
Async XLA Ops:
  7.2 25.7 %copy-start = (bf16[8,4,48,1024]{3,2,1,0:T(8,128)(2,1)S(1)}, bf16[8,4,48,1024]{3,2,1,0:T(8,128)(2,1)}, u32[]{:S(2)}) copy-start(bf16[8,4,48,1024]{3,2,1,0:T(8,128)(2,1)} %param.9) | copy-start | bytes 9437188
  33.9 0.9 copy-start.12
  34.8 16.3 %copy-start.10 = (bf16[32,8,256]{2,1,0:T(8,128)(2,1)S(1)}, bf16[32,8,256]{2,1,0:T(8,128)(2,1)}, u32[]{:S(2)}) copy-start(bf16[32,8,256]{2,1,0:T(8,128)(2,1)} %param.7) | copy-start | bytes 393220
  39.7 39.8 %all-to-all-start.2 = ((f32[32,32,1,256]{3,1,2,0:T(8,128)}), f32[32,32,1,256]{3,1,2,0:T(8,128)}, u32[]{:S(2)}, u32[]{:S(2)}) async-start(f32[32,32,1,256]{3,1,2,0:T(8,128)} %bitcast.189), calls=%async_computation.2 | async-start | bytes 2097152 | tf_op jit(solution)/shard_map/all_to_all | solution.py:46
  51.2 53.2 %copy-start.1 = (f32[32,8,256]{2,0,1:T(8,128)}, f32[32,8,256]{2,0,1:T(8,128)S(1)}, u32[]{:S(2)}) copy-start(f32[32,8,256]{2,0,1:T(8,128)S(1)} %copy_convert_fusion) | copy-start | bytes 786436
  80.8 23.6 %copy-start.5 = (f32[32,256]{1,0:T(8,128)}, f32[32,256]{1,0:T(8,128)S(1)}, u32[]{:S(2)}) copy-start(f32[32,256]{1,0:T(8,128)S(1)} %reduce_sum.45) | copy-start | bytes 98308
  116.5 0.7 copy-start.6
  144.1 17.0 %all-to-all-start.5 = ((bf16[32,12,256]{2,1,0:T(8,128)(2,1)}), bf16[32,12,256]{2,1,0:T(8,128)(2,1)S(1)}, u32[]{:S(2)}, u32[]{:S(2)}) async-start(bf16[32,12,256]{2,1,0:T(8,128)(2,1)} %broadcast_in_dim.25), calls=%async_computation.5 | async-start | bytes 524288 | tf_op jit(solution)/shard_map/all_to_all | solution.py:13
  161.1 15.0 %copy-start.3 = (bf16[32,12,256]{2,1,0:T(8,128)(2,1)}, bf16[32,12,256]{2,1,0:T(8,128)(2,1)S(1)}, u32[]{:S(2)}) copy-start(bf16[32,12,256]{2,1,0:T(8,128)(2,1)S(1)} %all-to-all-done.5) | copy-start | bytes 589828
  163.6 20.9 %all-to-all-start.6 = ((bf16[32,32,256]{2,1,0:T(8,128)(2,1)}), bf16[32,32,256]{2,1,0:T(8,128)(2,1)}, u32[]{:S(2)}, u32[]{:S(2)}) async-start(bf16[32,32,256]{2,1,0:T(8,128)(2,1)} %broadcast_in_dim.26), calls=%async_computation.6 | async-start | bytes 1048576 | tf_op jit(solution)/shard_map/all_to_all | solution.py:13
  168.2 214.8 %reduce-scatter.3.cloned.1.call-start = ((), (), s32[]{:S(2)}) async-start(), calls=%async_computation.17 | async-start | bytes 4128768 | tf_op jit(solution)/shard_map/reduce_scatter | solution.py:65
  198.5 0.6 copy-start.7
  231.4 17.4 %all-to-all-start.8 = ((bf16[32,12,256]{2,1,0:T(8,128)(2,1)}), bf16[32,12,256]{2,1,0:T(8,128)(2,1)S(1)}, u32[]{:S(2)}, u32[]{:S(2)}) async-start(bf16[32,12,256]{2,1,0:T(8,128)(2,1)} %broadcast_in_dim.27), calls=%async_computation.8 | async-start | bytes 524288 | tf_op jit(solution)/shard_map/all_to_all | solution.py:13
  248.8 23.6 %copy-start.4 = (bf16[32,12,256]{2,1,0:T(8,128)(2,1)}, bf16[32,12,256]{2,1,0:T(8,128)(2,1)S(1)}, u32[]{:S(2)}) copy-start(bf16[32,12,256]{2,1,0:T(8,128)(2,1)S(1)} %all-to-all-done.8) | copy-start | bytes 589828
  285.1 0.7 copy-start.8
  287.7 50.7 %slice-start = ((bf16[32,12,256]{2,1,0:T(8,128)(2,1)}), bf16[28,12,256]{2,1,0:T(8,128)(2,1)S(1)}, s32[]{:S(2)}) async-start(bf16[32,12,256]{2,1,0:T(8,128)(2,1)} %copy-done.3), calls=%async_computation.19 | async-start | bytes 458752 | tf_op jit(solution)/shard_map/slice | solution.py:103
  312.8 17.1 %all-to-all-start.11 = ((bf16[32,12,256]{2,1,0:T(8,128)(2,1)}), bf16[32,12,256]{2,1,0:T(8,128)(2,1)}, u32[]{:S(2)}, u32[]{:S(2)}) async-start(bf16[32,12,256]{2,1,0:T(8,128)(2,1)} %broadcast_in_dim.29), calls=%async_computation.11 | async-start | bytes 524288 | tf_op jit(solution)/shard_map/all_to_all | solution.py:13
  333.0 20.9 %all-to-all-start.12 = ((bf16[32,32,256]{2,1,0:T(8,128)(2,1)}), bf16[32,32,256]{2,1,0:T(8,128)(2,1)}, u32[]{:S(2)}, u32[]{:S(2)}) async-start(bf16[32,32,256]{2,1,0:T(8,128)(2,1)} %broadcast_in_dim.30), calls=%async_computation.12 | async-start | bytes 1048576 | tf_op jit(solution)/shard_map/all_to_all | solution.py:13
  368.0 0.7 copy-start.9
  370.6 23.0 %all-to-all-start.13 = ((f32[32,12,256]{2,1,0:T(8,128)}), f32[32,12,256]{2,1,0:T(8,128)}, u32[]{:S(2)}, u32[]{:S(2)}) async-start(f32[32,12,256]{2,1,0:T(8,128)} %reshape.100), calls=%async_computation.13 | async-start | bytes 1048576 | tf_op jit(solution)/shard_map/all_to_all | solution.py:46
  375.2 42.3 %reduce-scatter.5.cloned.1.call-start = ((), (), s32[]{:S(2)}) async-start(), calls=%async_computation.18 | async-start | bytes 573440 | tf_op jit(solution)/shard_map/reduce_scatter | solution.py:65
  377.1 39.7 %copy-start.11 = (f32[32,256]{1,0:T(8,128)S(1)}, f32[32,256]{1,0:T(8,128)}, u32[]{:S(2)}) copy-start(f32[32,256]{1,0:T(8,128)} %get-tuple-element.15) | copy-start | bytes 98308
  377.1 40.5 %copy-start.2 = (f32[32,8,256]{2,0,1:T(8,128)S(1)}, f32[32,8,256]{2,0,1:T(8,128)}, u32[]{:S(2)}) copy-start(f32[32,8,256]{2,0,1:T(8,128)} %copy-done.1) | copy-start | bytes 786436
  395.4 17.2 %all-to-all-start.14 = ((bf16[32,12,256]{2,1,0:T(8,128)(2,1)}), bf16[32,12,256]{2,1,0:T(8,128)(2,1)}, u32[]{:S(2)}, u32[]{:S(2)}) async-start(bf16[32,12,256]{2,1,0:T(8,128)(2,1)} %broadcast_in_dim.31), calls=%async_computation.14 | async-start | bytes 524288 | tf_op jit(solution)/shard_map/all_to_all | solution.py:13
Sparse Core Ops, SparseCore 0:
  176.2 62.7 reduce-scatter.2
  383.2 25.0 reduce-scatter.4
where the time goes:
time: 430 us; the launch traced here: 427 us
  blocking collectives  192 us (45%)
  waiting for transfers between devices  105 us (24%)
  starting transfers between devices  44.3 us (10%)
  matrix products  32.6 us (8%)
  local copies, waits for them, and re-layouts  32 us (7%)
  between operations  14.4 us (3%)
  other arithmetic  6.35 us (1%)
    all_to_all x3, blocking collectives, summed_on_arrival(): lax.all_to_all(cut_along(value, dim, count), axis, 0, 0, tiled=True)  74.9 us
    all_to_all x6, waiting for transfers between devices, copy_for_each(): lax.all_to_all(jnp.broadcast_to(value[None], (count, *value.shape)), axis...  69.7 us
    all_to_all x4, blocking collectives, copy_for_each(): lax.all_to_all(jnp.broadcast_to(value[None], (count, *value.shape)), axis...  67.2 us
    all_gather x4, blocking collectives, picked(): lax.all_gather(value, axis)  50.3 us
    all_to_all x2, waiting for transfers between devices, summed_on_arrival(): lax.all_to_all(cut_along(value, dim, count), axis, 0, 0, tiled=True)  34.8 us
    all_to_all x6, starting transfers between devices, copy_for_each(): lax.all_to_all(jnp.broadcast_to(value[None], (count, *value.shape)), axis...  28.2 us
    all_to_all x2, starting transfers between devices, summed_on_arrival(): lax.all_to_all(cut_along(value, dim, count), axis, 0, 0, tiled=True)  16.1 us
    slice x9, local copies, waits for them, and re-layouts, local(): all_coeff[1:]  10.6 us
  transfers between devices with their start and end apart: 10, of which 8 were waited for; matrix products, arithmetic and copies ran while one was open for 11% of the time, Pallas kernels for 0%

commit v1 on v0

v1 whole, which is shorter than its diff:
```python
import jax
import jax.numpy as jnp
from jax import lax
from jax.experimental import pallas as pl
from jax.experimental.pallas import tpu as pltpu
from jax.sharding import PartitionSpec as P

ROW = "row"
COL = "col"
CORES = 2
NX = 4
MESH = pl.DeviceIdType.MESH
F32 = jnp.float32
BF16 = jnp.bfloat16
GROUPS = ((0,), (1, 2, 3), (4, 5, 6, 7))


def remote(src, dst, send, recv, row, col):
    return pltpu.make_async_remote_copy(
        src_ref=src,
        dst_ref=dst,
        send_sem=send,
        recv_sem=recv,
        device_id={ROW: row, COL: col},
        device_id_type=MESH,
    )


def prior_kernel(left_in, right_in, known_in, out, left, right, known, coeff, *rest):
    rows, cols = lax.axis_size(ROW), lax.axis_size(COL)
    ny, nz = rows // CORES, cols // NX
    count = len(GROUPS)
    parts, from_a, from_b, from_l, from_r, part_sum, from_z = (
        rest[i * count : (i + 1) * count] for i in range(7)
    )
    local_sem, gather_send, gather_recv, x_send, x_recv, z_send, z_recv = rest[7 * count :]
    r, c = lax.axis_index(ROW), lax.axis_index(COL)
    y, q = r // CORES, r % CORES
    z, x = c // NX, c % NX
    up, down, far = (((y + d) % ny) * CORES + q for d in (1, ny - 1, 2))
    partner = y * CORES + 1 - q
    right_x, left_x, far_x = ((x + d) % NX for d in (1, NX - 1, 2))
    depth = known_in.shape[1]
    priors = known_in.shape[0]
    rank = left_in.shape[2]

    loads = [
        pltpu.make_async_copy(known_in, known.at[:, pl.ds(r * depth, depth)], local_sem.at[0]),
        pltpu.make_async_copy(right_in, right, local_sem.at[1]),
        pltpu.make_async_copy(left_in, left, local_sem.at[2]),
    ]
    for load in loads:
        load.start()
    barrier = pltpu.get_barrier_semaphore()
    peers = [(up, c), (down, c), (partner, c), (r, z * NX + right_x), (r, z * NX + left_x)]
    peers += [(r, ((z + d) % nz) * NX + x) for d in range(1, nz)]
    for row, col in peers:
        pl.semaphore_signal(barrier, inc=1, device_id={ROW: row, COL: col}, device_id_type=MESH)
    pl.semaphore_wait(barrier, len(peers))
    loads[0].wait()

    sends = []

    def go(copy):
        copy.start()
        sends.append(copy)
        return copy

    def block(row, j):
        return known.at[j, pl.ds(row * depth, depth)]

    def share(row_of_block, j, kind, target):
        return remote(
            block(row_of_block, j), block(row_of_block, j), gather_send.at[kind, j], gather_recv.at[kind, j], target, c
        )

    own_up, own_down, relay, over = [], [], [], [[], [], [], []]
    for j in range(priors):
        own_up.append(go(share(r, j, 0, up)))
        own_down.append(go(share(r, j, 1, down)))
        over[0].append(go(share(r, j, 3, partner)))
    for j in range(priors):
        own_up[j].wait_recv()
        over[1].append(go(share(down, j, 4, partner)))
        if j < priors // 2:
            relay.append(go(share(down, j, 2, up)))
        own_down[j].wait_recv()
        over[2].append(go(share(up, j, 5, partner)))
        if j >= priors // 2:
            relay.append(go(share(up, j, 2, down)))
    for load in loads[1:]:
        load.wait()
    for j in range(priors):
        relay[j].wait_recv()
        over[3].append(go(share(far, j, 6, partner)))
        for kind in range(4):
            over[kind][j].wait_recv()
        factors = right[:, j].reshape(-1, right.shape[3])
        product = jnp.dot(factors, known[j], preferred_element_type=F32)
        coeff[:, pl.ds(j * rank, rank)] = product.astype(BF16).reshape(-1, rank, product.shape[1])

    def multiply(g):
        first = GROUPS[g][0]

        def one(at, carry):
            a = at + first
            factors = left[a].reshape(priors * rank, -1)
            term = lax.dot_general(factors, coeff[a], (((0,), (0,)), ((), ())), preferred_element_type=F32)
            term = term.astype(BF16).reshape(nz, NX, -1, term.shape[1])
            for at_x in range(NX):
                parts[g][at_x, :, at] = term[:, at_x]
            return carry

        lax.fori_loop(0, len(GROUPS[g]), one, 0)

    low, high = pl.ds(0, nz // 2), pl.ds(nz // 2, nz // 2)
    steps = [dict() for _ in GROUPS]

    def send_x(g, kind, src, dst, target_x):
        return go(remote(src, dst, x_send.at[g, kind], x_recv.at[g, kind], r, z * NX + target_x))

    def x_first(g):
        steps[g]["a"] = send_x(g, 0, parts[g].at[far_x, low], from_a[g], right_x)
        steps[g]["b"] = send_x(g, 1, parts[g].at[far_x, high], from_b[g], left_x)
        steps[g]["l0"] = send_x(g, 2, parts[g].at[right_x, high], from_l[g].at[high], right_x)
        steps[g]["r0"] = send_x(g, 3, parts[g].at[left_x, low], from_r[g].at[low], left_x)

    def x_second(g):
        steps[g]["a"].wait_recv()
        parts[g][right_x, low] = (parts[g][right_x, low].astype(F32) + from_a[g][...].astype(F32)).astype(BF16)
        steps[g]["l1"] = send_x(g, 4, parts[g].at[right_x, low], from_l[g].at[low], right_x)
        steps[g]["b"].wait_recv()
        parts[g][left_x, high] = (parts[g][left_x, high].astype(F32) + from_b[g][...].astype(F32)).astype(BF16)
        steps[g]["r1"] = send_x(g, 5, parts[g].at[left_x, high], from_r[g].at[high], left_x)

    def z_all(g):
        for name in ("l0", "r0", "l1", "r1"):
            steps[g][name].wait_recv()

        def one(at, carry):
            total = parts[g][x, at].astype(F32) + from_l[g][at].astype(F32) + from_r[g][at].astype(F32)
            part_sum[g][at] = total.astype(BF16)
            return carry

        lax.fori_loop(0, nz, one, 0)
        steps[g]["z"] = []
        for d in range(1, nz):
            to = (z + d) % nz
            steps[g]["z"].append(
                go(remote(part_sum[g].at[to], from_z[g].at[d], z_send.at[g, d], z_recv.at[g, d], r, to * NX + x))
            )

    def finish(g):
        total = part_sum[g][z].astype(F32)
        for d in range(1, nz):
            steps[g]["z"][d - 1].wait_recv()
        for d in range(1, nz):
            total = total + from_z[g][d].astype(F32)
        out[pl.ds(GROUPS[g][0], len(GROUPS[g]))] = total

    multiply(0)
    x_first(0)
    multiply(1)
    x_first(1)
    x_second(0)
    multiply(2)
    x_first(2)
    z_all(0)
    x_second(1)
    finish(0)
    z_all(1)
    x_second(2)
    finish(1)
    z_all(2)
    finish(2)
    for copy in sends:
        copy.wait_send()


def prior_sums(prior_left, prior_right, solved_prior):
    local_rows, priors, rank, tile = prior_left.shape
    sides = solved_prior.shape[2]
    cols = lax.axis_size(COL)
    nz = cols // NX
    depth = tile // cols

    def buffers(*lead):
        return [pltpu.VMEM((*lead, len(group), depth, sides), BF16) for group in GROUPS]

    count = len(GROUPS)
    scratch = [
        pltpu.VMEM(prior_left.shape, BF16),
        pltpu.VMEM(prior_right.shape, BF16),
        pltpu.VMEM((priors, tile, sides), BF16),
        pltpu.VMEM((local_rows, priors * rank, sides), BF16),
        *buffers(NX, nz),
        *buffers(nz // 2),
        *buffers(nz // 2),
        *buffers(nz),
        *buffers(nz),
        *buffers(nz),
        *buffers(nz),
        pltpu.SemaphoreType.DMA((3,)),
        pltpu.SemaphoreType.DMA((7, priors)),
        pltpu.SemaphoreType.DMA((7, priors)),
        pltpu.SemaphoreType.DMA((count, 6)),
        pltpu.SemaphoreType.DMA((count, 6)),
        pltpu.SemaphoreType.DMA((count, nz)),
        pltpu.SemaphoreType.DMA((count, nz)),
    ]
    return pl.pallas_call(
        prior_kernel,
        out_shape=jax.ShapeDtypeStruct((local_rows, depth, sides), F32),
        in_specs=[pl.BlockSpec(memory_space=pl.ANY)] * 3,
        out_specs=pl.BlockSpec(memory_space=pltpu.VMEM),
        scratch_shapes=scratch,
        compiler_params=pltpu.CompilerParams(
            collective_id=0, has_side_effects=True, vmem_limit_bytes=48 * 1024 * 1024
        ),
    )(prior_left, prior_right, solved_prior)


def copy_for_each(value, axis):
    count = lax.axis_size(axis)
    return lax.all_to_all(
        jnp.broadcast_to(value[None], (count, *value.shape)), axis, 0, 0, tiled=True
    )


def laid_out(blocks, dim):
    lengths = list(blocks.shape[1:])
    lengths[dim] *= blocks.shape[0]
    return jnp.moveaxis(blocks, 0, dim).reshape(lengths)


def collect(value, axis, dim):
    return laid_out(copy_for_each(value, axis), dim)


def picked(value, axis, root):
    return lax.dynamic_index_in_dim(lax.all_gather(value, axis), root, 0, keepdims=False)


def cut_along(value, dim, count):
    before, after = (value.shape[:dim], value.shape[dim + 1 :])
    return jnp.moveaxis(value.reshape(*before, count, -1, *after), dim, 0)


def summed_on_arrival(value, axis, dim):
    count = lax.axis_size(axis)
    blocks = lax.all_to_all(cut_along(value, dim, count), axis, 0, 0, tiled=True)
    return jnp.sum(blocks, axis=0)


def padded_to(lines, count):
    spare = -len(lines) % count
    return jnp.pad(lines, [(0, spare)] + [(0, 0)] * (lines.ndim - 1))


def sum_by_parts(value, axes):
    lines = value.reshape(-1, value.shape[-1])
    own = summed_on_arrival(padded_to(lines, lax.axis_size(axes)), axes, 0)
    whole = collect(own, axes, 0)
    return whole[: len(lines)].reshape(value.shape)


def local(right_sides, prior_left, prior_right, solved_prior, diag_left, diag_right, diag_inverse):
    slice_rows = right_sides.shape[0]
    local_rows = right_sides.shape[1]
    sides_count = right_sides.shape[2]
    steps_count = diag_left.shape[1]
    row_index = lax.axis_index(ROW)
    prior = prior_sums(prior_left, prior_right, solved_prior)
    base = right_sides.astype(F32) - jnp.swapaxes(prior, 0, 1)
    leading = base[:, 0]
    solved_list = []
    trailing = jnp.zeros((slice_rows, local_rows - 1, sides_count), F32)
    for step in range(steps_count):
        block = diag_inverse[step]
        answer = jnp.dot(
            block, collect(leading.astype(BF16), COL, 0), preferred_element_type=F32
        ).astype(BF16)
        answer = picked(answer, ROW, step)
        solved_list.append(answer)
        all_terms = jnp.einsum("art,th->arh", diag_right[:, step], answer, preferred_element_type=F32)
        all_coeff = sum_by_parts(all_terms, COL).astype(BF16)
        first_coeff = all_coeff[0]
        trailing = trailing + jnp.einsum(
            "art,arh->tah", diag_left[1:, step], all_coeff[1:], preferred_element_type=F32
        )
        gate = (row_index > step).astype(F32)
        leading = leading - gate * jnp.einsum(
            "rt,rh->th", diag_left[0, step], first_coeff, preferred_element_type=F32
        )
    others = base[:, 1:] - trailing
    updated = jnp.concatenate([leading[:, None, :], others], axis=1)
    return (updated, jnp.stack(solved_list, 0))


def solution(mesh):
    return jax.shard_map(
        local,
        mesh=mesh,
        in_specs=(
            P(COL, ROW, None),
            P(ROW, COL, None, None),
            P(ROW, COL, None, None),
            P(COL, ROW, None),
            P(ROW, None, None, COL),
            P(ROW, None, None, COL),
            P(None, COL, None),
        ),
        out_specs=(P(COL, ROW, None), P(None, COL, None)),
        check_vma=False,
    )
```

time: 430 us -> 386 us (0.90)
  Pallas kernels: 0 us -> 81.3 us
  matrix products: 32.6 us -> 2.89 us
  local copies, waits for them, and re-layouts: 32 us -> 8.92 us
  waiting for transfers between devices: 105 us -> 82.8 us
  starting transfers between devices: 44.3 us -> 27.1 us
  between operations: 14.4 us -> 0.99 us
  blocking collectives: 192 us -> 180 us
  other arithmetic: 6.35 us -> 0.92 us
    pallas_call x0 -> x1, Pallas kernels: none -> 81.3 us  [prior_sums(): pl.pallas_call(prior_kernel, out_shape=jax.ShapeDtypeStruct((local_rows,...]
    all_to_all x2 -> x1, waiting for transfers between devices: 34.8 us -> 17.7 us  [summed_on_arrival(): lax.all_to_all(cut_along(value, dim, count), axis, 0, 0, tiled=True)]
    dot_general x7 -> x4, matrix products: 15.7 us -> 0.77 us  [local(): jnp.dot(block, collect(leading.astype(BF16), COL, 0), preferred_element_t...]
    all_to_all x2 -> x1, starting transfers between devices: 16.1 us -> 4.54 us  [summed_on_arrival(): lax.all_to_all(cut_along(value, dim, count), axis, 0, 0, tiled=True)]
    slice x9 -> x8, local copies, waits for them, and re-layouts: 10.6 us -> 0.24 us  [local(): all_coeff[1:]]
    all_to_all x3, blocking collectives: 74.9 us -> 67.7 us  [summed_on_arrival(): lax.all_to_all(cut_along(value, dim, count), axis, 0, 0, tiled=True)]
    dot_general x4, matrix products: 6.93 us -> 0.63 us  [local(): jnp.einsum('art,arh->tah', diag_left[1:, step], all_coeff[1:], preferred_...]
    all_to_all x6 -> x5, starting transfers between devices: 28.2 us -> 22.6 us  [copy_for_each(): lax.all_to_all(jnp.broadcast_to(value[None], (count, *value.shape)), axis...]
  transfers between devices with their start and end apart: 10 -> 6, of which waited for: 8 -> 6; matrix products, arithmetic and copies ran while one was open for 11% -> 0% of each run, Pallas kernels for 0% -> 0%
where the time goes in v1:
time: 386 us; the launch traced here: 385 us
  blocking collectives  180 us (47%)
  waiting for transfers between devices  82.8 us (21%)
  Pallas kernels  81.3 us (21%)
  starting transfers between devices  27.1 us (7%)
  local copies, waits for them, and re-layouts  8.92 us (2%)
    pallas_call x1, Pallas kernels, prior_sums(): pl.pallas_call(prior_kernel, out_shape=jax.ShapeDtypeStruct((local_rows,...  81.3 us
    all_to_all x3, blocking collectives, summed_on_arrival(): lax.all_to_all(cut_along(value, dim, count), axis, 0, 0, tiled=True)  67.7 us
    all_to_all x5, waiting for transfers between devices, copy_for_each(): lax.all_to_all(jnp.broadcast_to(value[None], (count, *value.shape)), axis...  65.1 us
    all_to_all x3, blocking collectives, copy_for_each(): lax.all_to_all(jnp.broadcast_to(value[None], (count, *value.shape)), axis...  62.3 us
    all_gather x4, blocking collectives, picked(): lax.all_gather(value, axis)  49.8 us
    all_to_all x5, starting transfers between devices, copy_for_each(): lax.all_to_all(jnp.broadcast_to(value[None], (count, *value.shape)), axis...  22.6 us
    all_to_all x1, waiting for transfers between devices, summed_on_arrival(): lax.all_to_all(cut_along(value, dim, count), axis, 0, 0, tiled=True)  17.7 us
  transfers between devices with their start and end apart: 6, of which 6 were waited for; matrix products, arithmetic and copies ran while one was open for 0% of the time, Pallas kernels for 0%

profile of v1, /device:TPU:8, one launch (start us, length us, event | category | flops | bytes accessed | tf_op | source)
XLA Modules:
  0.0 384.7 jit_solution(14465916479929800180)
XLA Ops:
  0.6 1.9 copy-done
  2.5 0.9 copy-done.1
  3.5 81.3 %shard_map.86 = f32[8,32,256]{2,1,0:T(8,128)S(1)} custom-call(bf16[8,4,48,1024]{3,2,1,0:T(8,128)(2,1)S(1)} %copy-done, bf16[8,4,48,1024]{3,2,1,0:T(8,128)(2,1)} %right_in.1, bf16[4,128,256]{2,1,0:T(8,128)(2,1)S(1)} %copy-done.1), custom_call_target="tpu_custom_call" | custom-call | tf_op jit(solution)/shard_map/pallas_call | solution.py:211
  84.9 21.6 %all_to_all.60 = bf16[32,32,256]{2,1,0:T(8,128)(2,1)S(1)} all-to-all(bf16[32,32,256]{2,1,0:T(8,128)(2,1)S(1)} %broadcast_in_dim.18), channel_id=1, replica_groups=mesh['row'=8,'col'=32] {'col'}, dimensions={0} | all-to-all | bytes 1048576 | tf_op jit(solution)/shard_map/all_to_all | solution.py:225
  106.8 11.5 %all-gather = bf16[256,256]{1,0:T(8,128)(2,1)S(1)} all-gather(bf16[32,256]{1,0:T(8,128)(2,1)S(1)} %fusion.11), channel_id=2, replica_groups=mesh['row'=8,'col'=32] {'row'}, dimensions={0}, use_global_device_ids=true | all-gather | bytes 147456 | tf_op jit(solution)/shard_map/all_gather | solution.py:241
  118.6 22.6 %all_to_all.61 = f32[32,12,256]{2,1,0:T(8,128)S(1)} all-to-all(f32[32,12,256]{2,1,0:T(8,128)S(1)} %reshape.65), channel_id=1, replica_groups=mesh['row'=8,'col'=32] {'col'}, dimensions={0} | all-to-all | bytes 786432 | tf_op jit(solution)/shard_map/all_to_all | solution.py:251
  141.2 0.7 broadcast_in_dim.19
  141.9 4.7 %all-to-all-start.2 = ((bf16[32,12,256]{2,1,0:T(8,128)(2,1)}), bf16[32,12,256]{2,1,0:T(8,128)(2,1)S(1)}, u32[]{:S(2)}, u32[]{:S(2)}) async-start(bf16[32,12,256]{2,1,0:T(8,128)(2,1)} %broadcast_in_dim.19), calls=%async_computation.2 | async-start | bytes 524288 | tf_op jit(solution)/shard_map/all_to_all | solution.py:225
  146.6 12.3 %all-to-all-done.2 = bf16[32,12,256]{2,1,0:T(8,128)(2,1)S(1)} async-done(((bf16[32,12,256]{2,1,0:T(8,128)(2,1)}), bf16[32,12,256]{2,1,0:T(8,128)(2,1)S(1)}, u32[]{:S(2)}, u32[]{:S(2)}) %all-to-all-start.2) | async-done | bytes 196640 | tf_op jit(solution)/shard_map/all_to_all | solution.py:225
  159.2 20.3 %all_to_all.62 = bf16[32,32,256]{2,1,0:T(8,128)(2,1)S(1)} all-to-all(bf16[32,32,256]{2,1,0:T(8,128)(2,1)S(1)} %broadcast_in_dim.20), channel_id=1, replica_groups=mesh['row'=8,'col'=32] {'col'}, dimensions={0} | all-to-all | bytes 1048576 | tf_op jit(solution)/shard_map/all_to_all | solution.py:225
  179.7 12.7 %all-gather.1 = bf16[256,256]{1,0:T(8,128)(2,1)S(1)} all-gather(bf16[32,256]{1,0:T(8,128)(2,1)S(1)} %fusion.12), channel_id=3, replica_groups=mesh['row'=8,'col'=32] {'row'}, dimensions={0}, use_global_device_ids=true | all-gather | bytes 147456 | tf_op jit(solution)/shard_map/all_gather | solution.py:241
  192.7 22.6 %all_to_all.63 = f32[32,12,256]{2,1,0:T(8,128)S(1)} all-to-all(f32[32,12,256]{2,1,0:T(8,128)S(1)} %reshape.67), channel_id=1, replica_groups=mesh['row'=8,'col'=32] {'col'}, dimensions={0} | all-to-all | bytes 786432 | tf_op jit(solution)/shard_map/all_to_all | solution.py:251
  215.4 0.7 broadcast_in_dim.21
  216.1 4.7 %all-to-all-start.5 = ((bf16[32,12,256]{2,1,0:T(8,128)(2,1)}), bf16[32,12,256]{2,1,0:T(8,128)(2,1)S(1)}, u32[]{:S(2)}, u32[]{:S(2)}) async-start(bf16[32,12,256]{2,1,0:T(8,128)(2,1)} %broadcast_in_dim.21), calls=%async_computation.5 | async-start | bytes 524288 | tf_op jit(solution)/shard_map/all_to_all | solution.py:225
  220.8 12.3 %all-to-all-done.5 = bf16[32,12,256]{2,1,0:T(8,128)(2,1)S(1)} async-done(((bf16[32,12,256]{2,1,0:T(8,128)(2,1)}), bf16[32,12,256]{2,1,0:T(8,128)(2,1)S(1)}, u32[]{:S(2)}, u32[]{:S(2)}) %all-to-all-start.5) | async-done | bytes 196640 | tf_op jit(solution)/shard_map/all_to_all | solution.py:225
  233.3 20.3 %all_to_all.64 = bf16[32,32,256]{2,1,0:T(8,128)(2,1)S(1)} all-to-all(bf16[32,32,256]{2,1,0:T(8,128)(2,1)S(1)} %broadcast_in_dim.22), channel_id=1, replica_groups=mesh['row'=8,'col'=32] {'col'}, dimensions={0} | all-to-all | bytes 1048576 | tf_op jit(solution)/shard_map/all_to_all | solution.py:225
  253.8 12.7 %all-gather.2 = bf16[256,256]{1,0:T(8,128)(2,1)S(1)} all-gather(bf16[32,256]{1,0:T(8,128)(2,1)S(1)} %fusion.13), channel_id=4, replica_groups=mesh['row'=8,'col'=32] {'row'}, dimensions={0}, use_global_device_ids=true | all-gather | bytes 147456 | tf_op jit(solution)/shard_map/all_gather | solution.py:241
  266.9 22.6 %all_to_all.65 = f32[32,12,256]{2,1,0:T(8,128)S(1)} all-to-all(f32[32,12,256]{2,1,0:T(8,128)S(1)} %reshape.69), channel_id=1, replica_groups=mesh['row'=8,'col'=32] {'col'}, dimensions={0} | all-to-all | bytes 786432 | tf_op jit(solution)/shard_map/all_to_all | solution.py:251
  289.5 0.7 broadcast_in_dim.23
  290.2 4.7 %all-to-all-start.8 = ((bf16[32,12,256]{2,1,0:T(8,128)(2,1)}), bf16[32,12,256]{2,1,0:T(8,128)(2,1)S(1)}, u32[]{:S(2)}, u32[]{:S(2)}) async-start(bf16[32,12,256]{2,1,0:T(8,128)(2,1)} %broadcast_in_dim.23), calls=%async_computation.8 | async-start | bytes 524288 | tf_op jit(solution)/shard_map/all_to_all | solution.py:225
  294.9 12.3 %all-to-all-done.8 = bf16[32,12,256]{2,1,0:T(8,128)(2,1)S(1)} async-done(((bf16[32,12,256]{2,1,0:T(8,128)(2,1)}), bf16[32,12,256]{2,1,0:T(8,128)(2,1)S(1)}, u32[]{:S(2)}, u32[]{:S(2)}) %all-to-all-start.8) | async-done | bytes 196640 | tf_op jit(solution)/shard_map/all_to_all | solution.py:225
  307.4 0.9 broadcast_in_dim.24
  308.2 3.9 %all-to-all-start.9 = ((bf16[32,32,256]{2,1,0:T(8,128)(2,1)}), bf16[32,32,256]{2,1,0:T(8,128)(2,1)S(1)}, u32[]{:S(2)}, u32[]{:S(2)}) async-start(bf16[32,32,256]{2,1,0:T(8,128)(2,1)} %broadcast_in_dim.24), calls=%async_computation.9 | async-start | bytes 1048576 | tf_op jit(solution)/shard_map/all_to_all | solution.py:225
  312.2 16.5 %all-to-all-done.9 = bf16[32,32,256]{2,1,0:T(8,128)(2,1)S(1)} async-done(((bf16[32,32,256]{2,1,0:T(8,128)(2,1)}), bf16[32,32,256]{2,1,0:T(8,128)(2,1)S(1)}, u32[]{:S(2)}, u32[]{:S(2)}) %all-to-all-start.9) | async-done | bytes 524320 | tf_op jit(solution)/shard_map/all_to_all | solution.py:225
  329.0 12.7 %all-gather.3 = bf16[256,256]{1,0:T(8,128)(2,1)S(1)} all-gather(bf16[32,256]{1,0:T(8,128)(2,1)S(1)} %fusion.14), channel_id=5, replica_groups=mesh['row'=8,'col'=32] {'row'}, dimensions={0}, use_global_device_ids=true | all-gather | bytes 147456 | tf_op jit(solution)/shard_map/all_gather | solution.py:241
  342.0 0.8 reshape.71
  342.8 4.5 %all-to-all-start.10 = ((f32[32,12,256]{2,1,0:T(8,128)}), f32[32,12,256]{2,1,0:T(8,128)S(1)}, u32[]{:S(2)}, u32[]{:S(2)}) async-start(f32[32,12,256]{2,1,0:T(8,128)} %reshape.71), calls=%async_computation.10 | async-start | bytes 1048576 | tf_op jit(solution)/shard_map/all_to_all | solution.py:251
  347.9 17.7 %all-to-all-done.10 = f32[32,12,256]{2,1,0:T(8,128)S(1)} async-done(((f32[32,12,256]{2,1,0:T(8,128)}), f32[32,12,256]{2,1,0:T(8,128)S(1)}, u32[]{:S(2)}, u32[]{:S(2)}) %all-to-all-start.10) | async-done | bytes 393248 | tf_op jit(solution)/shard_map/all_to_all | solution.py:251
  365.6 0.7 broadcast_in_dim.25
  366.4 4.7 %all-to-all-start.11 = ((bf16[32,12,256]{2,1,0:T(8,128)(2,1)}), bf16[32,12,256]{2,1,0:T(8,128)(2,1)S(1)}, u32[]{:S(2)}, u32[]{:S(2)}) async-start(bf16[32,12,256]{2,1,0:T(8,128)(2,1)} %broadcast_in_dim.25), calls=%async_computation.11 | async-start | bytes 524288 | tf_op jit(solution)/shard_map/all_to_all | solution.py:225
  371.9 11.5 %all-to-all-done.11 = bf16[32,12,256]{2,1,0:T(8,128)(2,1)S(1)} async-done(((bf16[32,12,256]{2,1,0:T(8,128)(2,1)}), bf16[32,12,256]{2,1,0:T(8,128)(2,1)S(1)}, u32[]{:S(2)}, u32[]{:S(2)}) %all-to-all-start.11) | async-done | bytes 196640 | tf_op jit(solution)/shard_map/all_to_all | solution.py:225
  383.8 0.9 copy.28
  (60 shorter events, 4.4 us)
Async XLA Ops:
  0.6 1.9 copy-start
  2.5 0.9 copy-start.1
  3.5 81.3 %copy-start.5 = (bf16[32,8,256]{2,1,0:T(8,128)(2,1)S(1)}, bf16[32,8,256]{2,1,0:T(8,128)(2,1)}, u32[]{:S(2)}) copy-start(bf16[32,8,256]{2,1,0:T(8,128)(2,1)} %param.7) | copy-start | bytes 393220
  3.5 103.1 %copy-start.3 = (bf16[4,32,1024]{2,1,0:T(8,128)(2,1)S(1)}, bf16[4,32,1024]{2,1,0:T(8,128)(2,1)}, u32[]{:S(2)}) copy-start(bf16[4,32,1024]{2,1,0:T(8,128)(2,1)} %param.13) | copy-start | bytes 786436
  3.5 114.8 %copy-start.4 = (bf16[8,4,48,32]{2,3,1,0:T(8,128)(2,1)S(1)}, bf16[8,4,48,32]{2,3,1,0:T(8,128)(2,1)}, u32[]{:S(2)}) copy-start(bf16[8,4,48,32]{2,3,1,0:T(8,128)(2,1)} %param.12) | copy-start | bytes 294916
  84.9 74.1 %copy-start.2 = (bf16[8,4,48,32]{2,3,1,0:T(8,128)(2,1)S(1)}, bf16[8,4,48,32]{2,3,1,0:T(8,128)(2,1)}, u32[]{:S(2)}) copy-start(bf16[8,4,48,32]{2,3,1,0:T(8,128)(2,1)} %param.11) | copy-start | bytes 294916
  141.9 17.0 %all-to-all-start.2 = ((bf16[32,12,256]{2,1,0:T(8,128)(2,1)}), bf16[32,12,256]{2,1,0:T(8,128)(2,1)S(1)}, u32[]{:S(2)}, u32[]{:S(2)}) async-start(bf16[32,12,256]{2,1,0:T(8,128)(2,1)} %broadcast_in_dim.19), calls=%async_computation.2 | async-start | bytes 524288 | tf_op jit(solution)/shard_map/all_to_all | solution.py:225
  216.1 17.0 %all-to-all-start.5 = ((bf16[32,12,256]{2,1,0:T(8,128)(2,1)}), bf16[32,12,256]{2,1,0:T(8,128)(2,1)S(1)}, u32[]{:S(2)}, u32[]{:S(2)}) async-start(bf16[32,12,256]{2,1,0:T(8,128)(2,1)} %broadcast_in_dim.21), calls=%async_computation.5 | async-start | bytes 524288 | tf_op jit(solution)/shard_map/all_to_all | solution.py:225
  290.2 17.0 %all-to-all-start.8 = ((bf16[32,12,256]{2,1,0:T(8,128)(2,1)}), bf16[32,12,256]{2,1,0:T(8,128)(2,1)S(1)}, u32[]{:S(2)}, u32[]{:S(2)}) async-start(bf16[32,12,256]{2,1,0:T(8,128)(2,1)} %broadcast_in_dim.23), calls=%async_computation.8 | async-start | bytes 524288 | tf_op jit(solution)/shard_map/all_to_all | solution.py:225
  308.2 20.5 %all-to-all-start.9 = ((bf16[32,32,256]{2,1,0:T(8,128)(2,1)}), bf16[32,32,256]{2,1,0:T(8,128)(2,1)S(1)}, u32[]{:S(2)}, u32[]{:S(2)}) async-start(bf16[32,32,256]{2,1,0:T(8,128)(2,1)} %broadcast_in_dim.24), calls=%async_computation.9 | async-start | bytes 1048576 | tf_op jit(solution)/shard_map/all_to_all | solution.py:225
  342.8 22.8 %all-to-all-start.10 = ((f32[32,12,256]{2,1,0:T(8,128)}), f32[32,12,256]{2,1,0:T(8,128)S(1)}, u32[]{:S(2)}, u32[]{:S(2)}) async-start(f32[32,12,256]{2,1,0:T(8,128)} %reshape.71), calls=%async_computation.10 | async-start | bytes 1048576 | tf_op jit(solution)/shard_map/all_to_all | solution.py:251
  366.4 17.0 %all-to-all-start.11 = ((bf16[32,12,256]{2,1,0:T(8,128)(2,1)}), bf16[32,12,256]{2,1,0:T(8,128)(2,1)S(1)}, u32[]{:S(2)}, u32[]{:S(2)}) async-start(bf16[32,12,256]{2,1,0:T(8,128)(2,1)} %broadcast_in_dim.25), calls=%async_computation.11 | async-start | bytes 524288 | tf_op jit(solution)/shard_map/all_to_all | solution.py:225

commit v2 on v0

v2 whole, which is shorter than its diff:
```python
import jax
import jax.numpy as jnp
from jax import lax
from jax.experimental import pallas as pl
from jax.experimental.pallas import tpu as pltpu
from jax.sharding import PartitionSpec as P

ROW = "row"
COL = "col"
CORES = 2
NX = 4
MESH = pl.DeviceIdType.MESH
F32 = jnp.float32
BF16 = jnp.bfloat16
LANES = 128
GROUPS = ((0,), (1, 2, 3), (4, 5, 6, 7))
LEAD_PAIRS = ((1, 0), (2, 0), (3, 0), (2, 1), (3, 1), (3, 2))
CROSS_PAIRS = ((2, 1), (3, 1), (3, 2))
CHUNK = 16
TN = (((0,), (0,)), ((), ()))
NT = (((1,), (1,)), ((), ()))


def dot(a, b, dims=None):
    if dims is None:
        return jnp.dot(a, b, preferred_element_type=F32)
    return lax.dot_general(a, b, dims, preferred_element_type=F32)


def remote(src, dst, send, recv, row, col):
    return pltpu.make_async_remote_copy(
        src_ref=src,
        dst_ref=dst,
        send_sem=send,
        recv_sem=recv,
        device_id={ROW: row, COL: col},
        device_id_type=MESH,
    )


class Place:
    def __init__(self):
        self.rows, self.cols = lax.axis_size(ROW), lax.axis_size(COL)
        self.ny, self.nz = self.rows // CORES, self.cols // NX
        self.r, self.c = lax.axis_index(ROW), lax.axis_index(COL)
        self.y, self.q = self.r // CORES, self.r % CORES
        self.z, self.x = self.c // NX, self.c % NX
        self.up, self.down, self.far = (((self.y + d) % self.ny) * CORES + self.q for d in (1, self.ny - 1, 2))
        self.partner = self.y * CORES + 1 - self.q
        self.right_x, self.left_x, self.far_x = ((self.x + d) % NX for d in (1, NX - 1, 2))
        self.low, self.high = pl.ds(0, self.nz // 2), pl.ds(self.nz // 2, self.nz // 2)
        self.sends = []

    def go(self, copy):
        copy.start()
        self.sends.append(copy)
        return copy

    def along_x(self, target):
        return self.z * NX + target

    def along_z(self, d):
        return ((self.z + d) % self.nz) * NX + self.x


class Reduce:
    def __init__(self, at, buffers, sems):
        self.at = at
        self.parts, self.from_a, self.from_b, self.from_l, self.from_r, self.part_sum, self.from_z = buffers
        self.x_send, self.x_recv, self.z_send, self.z_recv = sems
        self.copies = {}
        self.z_copies = []

    def send_x(self, kind, src, dst, target_x):
        at = self.at
        copy = remote(src, dst, self.x_send.at[kind], self.x_recv.at[kind], at.r, at.along_x(target_x))
        self.copies[kind] = at.go(copy)

    def first(self):
        at = self.at
        self.send_x(0, self.parts.at[at.far_x, at.low], self.from_a, at.right_x)
        self.send_x(1, self.parts.at[at.far_x, at.high], self.from_b, at.left_x)
        self.send_x(2, self.parts.at[at.right_x, at.high], self.from_l.at[at.high], at.right_x)
        self.send_x(3, self.parts.at[at.left_x, at.low], self.from_r.at[at.low], at.left_x)

    def second(self):
        at = self.at
        self.copies[0].wait_recv()
        own = self.parts[at.right_x, at.low].astype(F32)
        self.parts[at.right_x, at.low] = (own + self.from_a[...].astype(F32)).astype(BF16)
        self.send_x(4, self.parts.at[at.right_x, at.low], self.from_l.at[at.low], at.right_x)
        self.copies[1].wait_recv()
        own = self.parts[at.left_x, at.high].astype(F32)
        self.parts[at.left_x, at.high] = (own + self.from_b[...].astype(F32)).astype(BF16)
        self.send_x(5, self.parts.at[at.left_x, at.high], self.from_r.at[at.high], at.left_x)

    def third(self):
        at = self.at
        for kind in range(2, 6):
            self.copies[kind].wait_recv()

        def one(i, carry):
            total = self.parts[at.x, i].astype(F32) + self.from_l[i].astype(F32) + self.from_r[i].astype(F32)
            self.part_sum[i] = total.astype(BF16)
            return carry

        lax.fori_loop(0, at.nz, one, 0)
        for d in range(1, at.nz):
            src = self.part_sum.at[(at.z + d) % at.nz]
            copy = remote(src, self.from_z.at[d], self.z_send.at[d], self.z_recv.at[d], at.r, at.along_z(d))
            self.z_copies.append(at.go(copy))

    def result(self):
        at = self.at
        for copy in self.z_copies:
            copy.wait_recv()
        total = self.part_sum[at.z].astype(F32)
        for d in range(1, at.nz):
            total = total + self.from_z[d].astype(F32)
        return total


class Gather:
    def __init__(self, at, whole, sems):
        self.at = at
        self.whole = whole
        self.z_send, self.z_recv, self.x_send, self.x_recv = sems

    def z_copy(self, d):
        at = self.at
        own = self.whole.at[at.z, at.x]
        return remote(own, own, self.z_send.at[d], self.z_recv.at[d], at.r, at.along_z(d))

    def x_copy(self, kind):
        at, whole = self.at, self.whole
        part, target = (
            (whole.at[:, at.x], at.right_x),
            (whole.at[:, at.x], at.left_x),
            (whole.at[at.low, at.left_x], at.right_x),
            (whole.at[at.high, at.right_x], at.left_x),
        )[kind]
        return remote(part, part, self.x_send.at[kind], self.x_recv.at[kind], at.r, at.along_x(target))

    def first(self):
        for d in range(1, self.at.nz):
            self.z_copy(d).start()

    def second(self):
        for d in range(1, self.at.nz):
            self.z_copy(d).wait_recv()
        for kind in (0, 1):
            self.x_copy(kind).start()

    def third(self):
        for kind in (0, 1):
            self.x_copy(kind).wait_recv()
            self.x_copy(kind + 2).start()

    def wait(self):
        for kind in (2, 3):
            self.x_copy(kind).wait_recv()

    def close(self):
        for d in range(1, self.at.nz):
            self.z_copy(d).wait_send()
        for kind in range(4):
            self.x_copy(kind).wait_send()


def take(refs, count):
    return [refs.pop(0) for _ in range(count)]


def kernel(sides_in, left_in, right_in, known_in, dleft_in, dright_in, inverse_in, updated, solved, *scratch):
    at = Place()
    r, c, go = at.r, at.c, at.go
    refs = list(scratch)
    left, right, known, coeff, sides, dleft, dright, inverse = take(refs, 8)
    packs, lead_left, base_whole, near_whole, cross_whole = take(refs, 5)
    start, wide, lead_coeff, near = take(refs, 4)
    reduce_buffers = [take(refs, 7) for _ in range(len(GROUPS) + 2)]
    load_sem, gather_send, gather_recv, x_send, x_recv, z_send, z_recv = take(refs, 7)
    all_z_send, all_z_recv, all_x_send, all_x_recv = take(refs, 4)
    pack_send, pack_recv, start_send, start_recv = take(refs, 4)

    depth, priors = known_in.shape[1], known_in.shape[0]
    local_rows, steps, rank, thin = dleft.shape
    sides_count = sides.shape[2]
    tile = left.shape[3]
    width = steps * rank
    half = packs.shape[2] // 2

    def sems(i):
        return x_send.at[i], x_recv.at[i], z_send.at[i], z_recv.at[i]

    def all_sems(i):
        return all_z_send.at[i], all_z_recv.at[i], all_x_send.at[i], all_x_recv.at[i]

    prior = [Reduce(at, reduce_buffers[i], sems(i)) for i in range(len(GROUPS))]
    near_sum = Reduce(at, reduce_buffers[-2], sems(len(GROUPS)))
    cross_sum = Reduce(at, reduce_buffers[-1], sems(len(GROUPS) + 1))
    lead_all = Gather(at, lead_left, all_sems(0))
    base_all = Gather(at, base_whole, all_sems(1))
    near_all = Gather(at, near_whole, all_sems(2))
    cross_all = Gather(at, cross_whole, all_sems(3))

    loads = [
        pltpu.make_async_copy(src, dst, load_sem.at[i])
        for i, (src, dst) in enumerate(
            (
                (known_in, known.at[:, pl.ds(r * depth, depth)]),
                (dleft_in, dleft),
                (dright_in, dright),
                (right_in, right),
                (left_in, left),
                (inverse_in, inverse),
                (sides_in, sides),
            )
        )
    ]
    for load in loads:
        load.start()
    barrier = pltpu.get_barrier_semaphore()
    peers = [((r + d) % at.rows, c) for d in range(1, at.rows)]
    peers += [(r, at.along_x(at.right_x)), (r, at.along_x(at.left_x))]
    peers += [(r, at.along_z(d)) for d in range(1, at.nz)]
    for row, col in peers:
        pl.semaphore_signal(barrier, inc=1, device_id={ROW: row, COL: col}, device_id_type=MESH)

    for load in loads[1:3]:
        load.wait()
    eye = (
        lax.broadcasted_iota(jnp.int32, (thin, thin), 0) == lax.broadcasted_iota(jnp.int32, (thin, thin), 1)
    ).astype(BF16)
    packs[r] = jnp.zeros(packs.shape[1:], BF16)
    packs[r, :, :width] = dot(eye, dleft[0].reshape(width, thin), NT).astype(BF16)
    packs[r, :, half : half + width] = dot(eye, dright[0].reshape(width, thin), NT).astype(BF16)
    loads[0].wait()
    pl.semaphore_wait(barrier, len(peers))

    def block(row, j):
        return known.at[j, pl.ds(row * depth, depth)]

    def share(row_of_block, j, kind, target):
        part = block(row_of_block, j)
        return remote(part, part, gather_send.at[kind, j], gather_recv.at[kind, j], target, c)

    own_up, own_down, relay, over = [], [], [], [[], [], [], []]
    for j in range(priors):
        own_up.append(go(share(r, j, 0, at.up)))
        own_down.append(go(share(r, j, 1, at.down)))
        over[0].append(go(share(r, j, 3, at.partner)))
    pack_copies = [
        go(remote(packs.at[r], packs.at[r], pack_send.at[d], pack_recv.at[d], (r + d) % at.rows, c))
        for d in range(1, at.rows)
    ]
    for j in range(priors):
        own_up[j].wait_recv()
        over[1].append(go(share(at.down, j, 4, at.partner)))
        if j < priors // 2:
            relay.append(go(share(at.down, j, 2, at.up)))
        own_down[j].wait_recv()
        over[2].append(go(share(at.up, j, 5, at.partner)))
        if j >= priors // 2:
            relay.append(go(share(at.up, j, 2, at.down)))

    for copy in pack_copies:
        copy.wait_recv()
    firsts = (None, 0, LANES, 2 * LANES)
    lead_left[at.z, at.x] = jnp.zeros(lead_left.shape[2:], BF16)
    for k in range(1, steps):
        lead_left[at.z, at.x, :, firsts[k] : firsts[k] + k * rank] = packs[k, :, : k * rank]
    lead_all.first()

    for load in loads[3:]:
        load.wait()
    for j in range(priors):
        relay[j].wait_recv()
        over[3].append(go(share(at.far, j, 6, at.partner)))
        for kind in range(4):
            over[kind][j].wait_recv()
        product = dot(right[:, j].reshape(-1, tile), known[j])
        coeff[:, pl.ds(j * rank, rank)] = product.astype(BF16).reshape(local_rows, rank, sides_count)

    def multiply(g):
        first = GROUPS[g][0]

        def one(i, carry):
            term = dot(left[i + first].reshape(priors * rank, tile), coeff[i + first], TN)
            term = term.astype(BF16).reshape(at.nz, NX, thin, sides_count)
            for at_x in range(NX):
                prior[g].parts[at_x, :, i] = term[:, at_x]
            return carry

        lax.fori_loop(0, len(GROUPS[g]), one, 0)

    def own_base(g):
        total = prior[g].result()
        for i, a in enumerate(GROUPS[g]):
            updated[a] = sides[a].astype(F32) - total[i]

    multiply(0)
    prior[0].first()
    lead_all.second()
    multiply(1)
    prior[0].second()
    lead_all.third()
    prior[1].first()
    prior[0].third()
    lead_all.wait()

    def lanes_of(m):
        return slice(firsts[m], firsts[m] + (LANES if m < 3 else 2 * LANES))

    whole_left = lead_left[...].reshape(tile, lead_left.shape[3])
    for m in range(1, steps):
        wide[:, lanes_of(m)] = dot(inverse[m], whole_left[:, lanes_of(m)]).astype(BF16)
    own_base(0)

    @pl.when(r < steps)
    def _():
        base_whole[at.z, at.x] = updated[0].astype(BF16)
        base_all.first()

    for m in range(1, steps):
        product = dot(dright[:, m].reshape(local_rows * rank, thin), wide[:, lanes_of(m)])
        product = product.astype(BF16).reshape(local_rows, rank, -1)
        cross_sum.parts[m, :, :rank] = product[:, :, :LANES]
        if m == 3:
            cross_sum.parts[0, :, :rank] = product[:, :, LANES:]

    def spread(target, pairs, right_of):
        chunks = []
        for k, m in pairs:
            factors = packs[k, :, half : half + width]
            product = dot(factors, right_of(m), TN)[m * rank : (m + 1) * rank]
            chunks += [product[i : i + CHUNK] for i in range(0, rank, CHUNK)]
        for i in range(at.cols):
            part = chunks[i].astype(BF16) if i < len(chunks) else jnp.zeros((CHUNK, target.parts.shape[3]), BF16)
            target.parts[i % NX, i // NX, rank:] = part

    spread(cross_sum, CROSS_PAIRS, lambda m: wide[:, lanes_of(m)])
    cross_sum.first()

    @pl.when(r < steps)
    def _():
        base_all.second()

    cross_sum.second()

    @pl.when(r < steps)
    def _():
        base_all.third()

    multiply(2)

    def start_copy(k, d):
        return remote(start.at[k], start.at[k], start_send.at[d], start_recv.at[k], (r + d) % at.rows, c)

    @pl.when(r < steps)
    def _():
        base_all.wait()
        start[r] = dot(inverse[r], base_whole[...].reshape(tile, sides_count)).astype(BF16)
        for d in range(1, at.rows):
            start_copy(r, d).start()

    cross_sum.third()
    prior[2].first()
    prior[1].second()
    for k in range(steps):

        @pl.when(r != k)
        def _():
            start_copy(k, 1).wait_recv()

    for m in range(steps):
        product = dot(dright[:, m].reshape(local_rows * rank, thin), start[m])
        near_sum.parts[m, :, :rank] = product.astype(BF16).reshape(local_rows, rank, sides_count)
    spread(near_sum, LEAD_PAIRS, lambda m: start[m])
    near_sum.first()
    cross_whole[at.z, at.x] = cross_sum.result().astype(BF16)
    cross_all.first()
    near_sum.second()
    prior[1].third()
    prior[2].second()
    cross_all.second()
    near_sum.third()
    cross_all.third()
    near_whole[at.z, at.x] = near_sum.result().astype(BF16)
    near_all.first()
    own_base(1)
    prior[2].third()
    near_all.second()
    near_all.third()
    own_base(2)
    cross_all.wait()
    near_all.wait()

    def lead_rows(whole, i):
        return jnp.concatenate(
            [whole[(3 * i + n) // NX, (3 * i + n) % NX, rank:].astype(F32) for n in range(3)], axis=0
        )

    for m in range(1, steps):
        lead_coeff[m] = jnp.zeros(lead_coeff.shape[1:], BF16)
    for i, (k, m) in enumerate(LEAD_PAIRS):
        value = lead_rows(near_whole, i)
        if m:
            cross = lead_rows(cross_whole, CROSS_PAIRS.index((k, m))).astype(BF16)
            value = value - dot(cross, lead_coeff[m, :LANES])
        lead_coeff[k, m * rank : (m + 1) * rank] = value.astype(BF16)

    for m in range(steps):
        answer = start[m].astype(F32)
        terms = near_whole[:, m, :rank].reshape(local_rows * rank, sides_count).astype(F32)
        if m:
            lanes = LANES if m < 3 else 2 * LANES
            answer = answer - dot(wide[:, lanes_of(m)], lead_coeff[m, :lanes])
            cross = cross_whole[:, m, :rank].reshape(local_rows * rank, LANES)
            terms = terms - dot(cross, lead_coeff[m, :LANES])
            if m == 3:
                cross = cross_whole[:, 0, :rank].reshape(local_rows * rank, LANES)
                terms = terms - dot(cross, lead_coeff[m, LANES:])
        solved[m] = answer.astype(BF16)
        near[:, m * rank : (m + 1) * rank] = terms.astype(BF16).reshape(local_rows, rank, sides_count)
    for m in range(steps):

        @pl.when(r <= m)
        def _():
            near[0, m * rank : (m + 1) * rank] = jnp.zeros((rank, sides_count), BF16)

    def last(a, carry):
        updated[a] = updated[a] - dot(dleft[a].reshape(width, thin), near[a], TN)
        return carry

    lax.fori_loop(0, local_rows, last, 0)

    for copy in at.sends:
        copy.wait_send()
    for gather in (lead_all, near_all, cross_all):
        gather.close()

    @pl.when(r < steps)
    def _():
        base_all.close()
        for d in range(1, at.rows):
            start_copy(r, d).wait_send()


def local(right_sides, prior_left, prior_right, solved_prior, diag_left, diag_right, diag_inverse):
    thin, local_rows, sides = right_sides.shape
    priors, rank, tile = prior_left.shape[1:]
    steps = diag_left.shape[1]
    rows, cols = lax.axis_size(ROW), lax.axis_size(COL)
    nz = cols // NX
    block = rank + CHUNK

    def reduce_scratch(*shape):
        return [
            pltpu.VMEM((*lead, *shape), BF16)
            for lead in ((NX, nz), (nz // 2,), (nz // 2,), (nz,), (nz,), (nz,), (nz,))
        ]

    count = len(GROUPS) + 2
    scratch = [
        pltpu.VMEM(prior_left.shape, BF16),
        pltpu.VMEM(prior_right.shape, BF16),
        pltpu.VMEM((priors, tile, sides), BF16),
        pltpu.VMEM((local_rows, priors * rank, sides), BF16),
        pltpu.VMEM((local_rows, thin, sides), BF16),
        pltpu.VMEM(diag_left.shape, BF16),
        pltpu.VMEM(diag_right.shape, BF16),
        pltpu.VMEM(diag_inverse.shape, BF16),
        pltpu.VMEM((rows, thin, 4 * LANES), BF16),
        pltpu.VMEM((nz, NX, thin, 4 * LANES), BF16),
        pltpu.VMEM((nz, NX, thin, sides), BF16),
        pltpu.VMEM((nz, NX, block, sides), BF16),
        pltpu.VMEM((nz, NX, block, LANES), BF16),
        pltpu.VMEM((steps, thin, sides), BF16),
        pltpu.VMEM((thin, 4 * LANES), BF16),
        pltpu.VMEM((steps, 2 * LANES, sides), BF16),
        pltpu.VMEM((local_rows, steps * rank, sides), BF16),
    ]
    for group in GROUPS:
        scratch += reduce_scratch(len(group), thin, sides)
    scratch += reduce_scratch(block, sides)
    scratch += reduce_scratch(block, LANES)
    for shape in (
        (7,),
        (7, priors),
        (7, priors),
        (count, 6),
        (count, 6),
        (count, nz),
        (count, nz),
        (4, nz),
        (4, nz),
        (4, 4),
        (4, 4),
        (rows,),
        (rows,),
        (rows,),
        (steps,),
    ):
        scratch.append(pltpu.SemaphoreType.DMA(shape))
    updated, solved = pl.pallas_call(
        kernel,
        out_shape=(
            jax.ShapeDtypeStruct((local_rows, thin, sides), F32),
            jax.ShapeDtypeStruct((steps, thin, sides), BF16),
        ),
        in_specs=[pl.BlockSpec(memory_space=pl.ANY)] * 7,
        out_specs=(pl.BlockSpec(memory_space=pltpu.VMEM), pl.BlockSpec(memory_space=pltpu.VMEM)),
        scratch_shapes=scratch,
        compiler_params=pltpu.CompilerParams(
            collective_id=0, has_side_effects=True, vmem_limit_bytes=56 * 1024 * 1024
        ),
    )(
        jnp.swapaxes(right_sides, 0, 1),
        prior_left,
        prior_right,
        solved_prior,
        diag_left,
        diag_right,
        diag_inverse,
    )
    return jnp.swapaxes(updated, 0, 1), solved


def solution(mesh):
    return jax.shard_map(
        local,
        mesh=mesh,
        in_specs=(
            P(COL, ROW, None),
            P(ROW, COL, None, None),
            P(ROW, COL, None, None),
            P(COL, ROW, None),
            P(ROW, None, None, COL),
            P(ROW, None, None, COL),
            P(None, COL, None),
        ),
        out_specs=(P(COL, ROW, None), P(None, COL, None)),
        check_vma=False,
    )
```

time: 430 us -> 133 us (0.31)
  blocking collectives: 192 us -> 0 us
  Pallas kernels: 0 us -> 123 us
  waiting for transfers between devices: 105 us -> 0 us
  starting transfers between devices: 44.3 us -> 0 us
  matrix products: 32.6 us -> 0 us
  local copies, waits for them, and re-layouts: 32 us -> 8.61 us
  between operations: 14.4 us -> 0.64 us
  other arithmetic: 6.35 us -> 0 us
    all_to_all x7 -> x0, blocking collectives: 142 us -> none  [the longest x3 74.9 us: summed_on_arrival(): lax.all_to_all(cut_along(value, dim, count), axis, 0, 0, tiled=True)]
    pallas_call x0 -> x1, Pallas kernels: none -> 123 us  [local(): pl.pallas_call(kernel, out_shape=(jax.ShapeDtypeStruct((local_rows, thin,...]
    all_to_all x8 -> x0, waiting for transfers between devices: 104 us -> none  [the longest x6 69.7 us: copy_for_each(): lax.all_to_all(jnp.broadcast_to(value[None], (count, *value.shape)), axis...]
    all_gather x4 -> x0, blocking collectives: 50.3 us -> none  [picked(): lax.all_gather(value, axis)]
    all_to_all x8 -> x0, starting transfers between devices: 44.2 us -> none  [the longest x6 28.2 us: copy_for_each(): lax.all_to_all(jnp.broadcast_to(value[None], (count, *value.shape)), axis...]
    dot_general x19 -> x0, matrix products: 32.6 us -> none  [the longest x2 10.1 us: prior_term(): jnp.einsum('aprt,aprh->tah', left_block, coeff_block, preferred_element_t...]
    slice x13 -> x0, local copies, waits for them, and re-layouts: 12.1 us -> none  [the longest x9 10.6 us: local(): all_coeff[1:]]
    broadcast_in_dim x10 -> x0, local copies, waits for them, and re-layouts: 6.14 us -> none  [copy_for_each(): jnp.broadcast_to(value[None], (count, *value.shape))]
  transfers between devices with their start and end apart: 10 -> 0, of which waited for: 8 -> 0; matrix products, arithmetic and copies ran while one was open for 11% -> 0% of each run, Pallas kernels for 0% -> 0%
where the time goes in v2:
time: 133 us; the launch traced here: 132 us
  Pallas kernels  123 us (92%)
  local copies, waits for them, and re-layouts  8.61 us (6%)
    pallas_call x1, Pallas kernels, local(): pl.pallas_call(kernel, out_shape=(jax.ShapeDtypeStruct((local_rows, thin,...  123 us
    unnamed x5, local copies, waits for them, and re-layouts  8.61 us

profile of v2, /device:TPU:8, one launch (start us, length us, event | category | flops | bytes accessed | tf_op | source)
XLA Modules:
  0.0 132.4 jit_solution(13234596416604446505)
XLA Ops:
  0.6 1.6 %copy.14 = bf16[32,8,256]{2,0,1:T(8,128)(2,1)} copy(bf16[32,8,256]{2,1,0:T(8,128)(2,1)} %param.7) | data formatting | bytes 262144 | tf_op args[0]
  2.2 1.9 %copy.10.dleft_in = bf16[8,4,48,32]{3,2,1,0:T(8,128)(2,1)} copy(bf16[8,4,48,32]{2,3,1,0:T(8,128)(2,1)} %param.11) | data formatting | bytes 196608 | tf_op args[4]
  4.1 1.9 %copy.11.dright_in = bf16[8,4,48,32]{3,2,1,0:T(8,128)(2,1)} copy(bf16[8,4,48,32]{2,3,1,0:T(8,128)(2,1)} %param.12) | data formatting | bytes 196608 | tf_op args[5]
  6.0 123.1 %shard_map.86 = (f32[8,32,256]{2,1,0:T(8,128)}, bf16[4,32,256]{2,1,0:T(8,128)(2,1)}) custom-call(bf16[8,32,256]{2,1,0:T(8,128)(2,1)} %bitcast.4, bf16[8,4,48,1024]{3,2,1,0:T(8,128)(2,1)} %left_in.1, bf16[8,4,48,1024]{3,2,1,0:T(8,128)(2,1)} %right_in.1, bf16[4,128,256]{2,1,0:T(8,128)(2,1)} %known_in.1, bf16[8,4,48,32]{3,2,1,0:T(8,128)(2,1)} %copy.10.dleft_in, ...), custom_call_target="tpu_custom_call" | custom-call | tf_op jit(solution)/shard_map/pallas_call | solution.py:506
  129.1 1.8 %copy.12 = f32[32,8,256]{2,1,0:T(8,128)} copy(f32[32,8,256]{2,0,1:T(8,128)} %bitcast.5) | data formatting | bytes 524288
  130.9 1.5 %copy.16 = bf16[4,32,256]{2,1,0:T(8,128)(2,1)} copy(bf16[4,32,256]{2,1,0:T(8,128)(2,1)} %get-tuple-element.11) | data formatting | bytes 131072

commit v3 on v2

v3 whole, which is shorter than its diff:
```python
import jax
import jax.numpy as jnp
from jax import lax
from jax.experimental import pallas as pl
from jax.experimental.pallas import tpu as pltpu
from jax.sharding import PartitionSpec as P

ROW = "row"
COL = "col"
CORES = 2
NX = 4
MESH = pl.DeviceIdType.MESH
F32 = jnp.float32
BF16 = jnp.bfloat16
LANES = 128
GROUPS = ((0,), (1, 2, 3), (4, 5, 6, 7))
CHUNK = 24
TN = (((0,), (0,)), ((), ()))


def dot(a, b, dims=None):
    if dims is None:
        return jnp.dot(a, b, preferred_element_type=F32)
    return lax.dot_general(a, b, dims, preferred_element_type=F32)


def remote(src, dst, send, recv, row, col):
    return pltpu.make_async_remote_copy(
        src_ref=src,
        dst_ref=dst,
        send_sem=send,
        recv_sem=recv,
        device_id={ROW: row, COL: col},
        device_id_type=MESH,
    )


class Copy:
    def __init__(self, copy, only=None):
        self.copy, self.only, self.landed = copy, only, False

    def wait_recv(self):
        self.copy.wait_recv()
        self.landed = True

    def close(self):
        def rest():
            if not self.landed:
                self.copy.wait_recv()
            self.copy.wait_send()

        if self.only is None:
            rest()
        else:
            pl.when(self.only)(rest)


class Place:
    def __init__(self):
        self.rows, self.cols = lax.axis_size(ROW), lax.axis_size(COL)
        self.ny, self.nz = self.rows // CORES, self.cols // NX
        self.r, self.c = lax.axis_index(ROW), lax.axis_index(COL)
        self.y, self.q = self.r // CORES, self.r % CORES
        self.z, self.x = self.c // NX, self.c % NX
        self.up, self.down, self.far = (((self.y + d) % self.ny) * CORES + self.q for d in (1, self.ny - 1, 2))
        self.partner = self.y * CORES + 1 - self.q
        self.next_x = [(self.x + d) % NX for d in range(NX)]
        self.along_x = [self.z * NX + to for to in self.next_x]
        self.low, self.high = pl.ds(0, self.nz // 2), pl.ds(self.nz // 2, self.nz // 2)
        self.next_z = [(self.z + d) % self.nz for d in range(self.nz)]
        self.along_z = [to * NX + self.x for to in self.next_z]
        self.next_r = [(self.r + d) % self.rows for d in range(self.rows)]
        self.sends = []

    def go(self, copy, only=None):
        copy.start()
        tracked = Copy(copy, only)
        self.sends.append(tracked)
        return tracked

    def start(self, copies, only=None):
        return [self.go(copy, only) for copy in copies]

    def to_all_x(self, src, dst, sems):
        send, recv = sems
        return [
            remote(src(self.next_x[d]), dst(d), send.at[d], recv.at[d], self.r, self.along_x[d]) for d in (1, 3, 2)
        ]

    def to_all_z(self, src, dst, sems):
        send, recv = sems
        order = [4, 3, 5, 2, 6, 1, 7] if self.nz == 8 else range(1, self.nz)
        return [
            remote(src(self.next_z[d]), dst(d), send.at[d], recv.at[d], self.r, self.along_z[d]) for d in order
        ]


def landed(copies):
    for copy in copies:
        copy.wait_recv()


class Reduce:
    def __init__(self, at, buffers, x_sems, z_sems):
        self.at = at
        self.parts, self.from_a, self.from_b, self.from_l, self.from_r, self.part_sum, self.from_z = buffers
        self.x_send, self.x_recv = x_sems
        self.z_sems = z_sems
        self.copies = {}

    def send_x(self, kind, src, dst, d):
        at = self.at
        copy = remote(src, dst, self.x_send.at[kind], self.x_recv.at[kind], at.r, at.along_x[d])
        self.copies[kind] = at.go(copy)

    def first(self):
        at = self.at
        left, right, far = at.next_x[3], at.next_x[1], at.next_x[2]
        self.send_x(0, self.parts.at[far, at.low], self.from_a, 1)
        self.send_x(1, self.parts.at[far, at.high], self.from_b, 3)
        self.send_x(2, self.parts.at[right, at.high], self.from_l.at[at.high], 1)
        self.send_x(3, self.parts.at[left, at.low], self.from_r.at[at.low], 3)

    def second(self):
        at = self.at
        left, right = at.next_x[3], at.next_x[1]
        self.copies[0].wait_recv()
        own = self.parts[right, at.low].astype(F32)
        self.parts[right, at.low] = (own + self.from_a[...].astype(F32)).astype(BF16)
        self.send_x(4, self.parts.at[right, at.low], self.from_l.at[at.low], 1)
        self.copies[1].wait_recv()
        own = self.parts[left, at.high].astype(F32)
        self.parts[left, at.high] = (own + self.from_b[...].astype(F32)).astype(BF16)
        self.send_x(5, self.parts.at[left, at.high], self.from_r.at[at.high], 3)

    def third(self):
        at = self.at
        for kind in range(2, 6):
            self.copies[kind].wait_recv()

        def one(i, carry):
            total = self.parts[at.x, i].astype(F32) + self.from_l[i].astype(F32) + self.from_r[i].astype(F32)
            self.part_sum[i] = total.astype(BF16)
            return carry

        lax.fori_loop(0, at.nz, one, 0)
        self.send_z()

    def send_z(self):
        at = self.at
        self.z_copies = at.start(
            at.to_all_z(lambda to: self.part_sum.at[to], lambda d: self.from_z.at[d], self.z_sems)
        )

    def result(self):
        at = self.at
        landed(self.z_copies)
        total = self.part_sum[at.z].astype(F32)
        for d in range(1, at.nz):
            total = total + self.from_z[d].astype(F32)
        return total


class ReduceDirect(Reduce):
    def __init__(self, at, buffers, x_sems, z_sems):
        self.at = at
        self.parts, self.from_x, self.part_sum, self.from_z = buffers
        self.x_sems, self.z_sems = x_sems, z_sems

    def first(self):
        at = self.at
        self.x_copies = at.start(
            at.to_all_x(lambda to: self.parts.at[to], lambda d: self.from_x.at[d - 1], self.x_sems)
        )

    def second(self):
        at = self.at
        landed(self.x_copies)

        def one(i, carry):
            total = self.parts[at.x, i].astype(F32)
            for d in range(NX - 1):
                total = total + self.from_x[d, i].astype(F32)
            self.part_sum[i] = total.astype(BF16)
            return carry

        lax.fori_loop(0, at.nz, one, 0)
        self.send_z()


class Gather:
    def __init__(self, at, whole, x_sems, z_sems, only=None):
        self.at, self.whole, self.only = at, whole, only
        self.z_made = at.to_all_z(lambda to: whole.at[at.z, at.x], lambda d: whole.at[at.z, at.x], z_sems)
        self.x_made = at.to_all_x(lambda to: whole.at[:, at.x], lambda d: whole.at[:, at.x], x_sems)

    def first(self):
        self.z_copies = self.at.start(self.z_made, self.only)

    def second(self):
        landed(self.z_copies)
        self.x_copies = self.at.start(self.x_made, self.only)

    def wait(self):
        landed(self.x_copies)


class Flow:
    def __init__(self, at, buffers, sems, separate):
        self.at, self.separate = at, separate
        self.source, self.block, self.parts, self.from_z, self.steps, self.lead, self.out, self.whole = buffers
        self.sems = sems

    def feed(self):
        at = self.at
        self.block[at.x] = self.source[at.x]
        self.fed = at.start(
            at.to_all_x(lambda to: self.source.at[to], lambda d: self.block.at[at.x], self.sems[0])
        )

    def right(self, factors, positions, rank):
        at = self.at
        landed(self.fed)
        count, thin, sides = self.block.shape
        product = dot(factors[...].reshape(count * thin, -1), self.block[...].reshape(count * thin, sides), TN)
        self.parts[:, :rank] = product[: positions * rank].astype(BF16).reshape(positions, rank, sides)
        lead = product[positions * rank :]
        chunks = (NX - 1) * rank // CHUNK
        for i in range(at.nz):
            part = lead[i * CHUNK : (i + 1) * CHUNK] if i < chunks else jnp.zeros((CHUNK, sides), F32)
            self.parts[i, rank:] = part.astype(BF16)
        self.z_copies = at.start(
            at.to_all_z(lambda to: self.parts.at[to], lambda d: self.from_z.at[d], self.sems[1])
        )

    def share(self, rank, off):
        at = self.at
        landed(self.z_copies)
        total = self.parts[at.z].astype(F32)
        for d in range(1, at.nz):
            total = total + self.from_z[d].astype(F32)
        self.steps[at.x] = jnp.where(off, 0.0, total[:rank]).astype(BF16)
        self.lead[at.x, at.z] = total[rank:].astype(BF16)
        self.x_copies = at.start(
            at.to_all_x(lambda to: self.steps.at[at.x], lambda d: self.steps.at[at.x], self.sems[2])
        )
        own = self.lead.at[at.x, at.z]
        self.lead_z = at.start(at.to_all_z(lambda to: own, lambda d: own, self.sems[3]))

    def left(self, factors):
        at = self.at
        landed(self.x_copies)
        nz, thin, width = factors.shape
        rows = factors[...].reshape(nz * thin, width)
        rank = self.steps.shape[1]
        if self.separate:
            for m in range(1, NX):
                lanes = lanes_of(m)
                product = dot(rows[:, m * rank : (m + 1) * rank], self.steps[m, :, : lanes.stop - lanes.start])
                self.out[:, :, lanes] = product.astype(BF16).reshape(nz, thin, -1)
        else:
            product = dot(rows, self.steps[...].reshape(width, -1))
            self.out[...] = product.astype(BF16).reshape(nz, thin, -1)
        self.whole[at.z] = self.out[at.z]
        self.out_copies = at.start(
            at.to_all_z(lambda to: self.out.at[to], lambda d: self.whole.at[at.z], self.sems[4])
        )

    def lead_x(self):
        at = self.at
        landed(self.lead_z)
        own = self.lead.at[at.x]
        self.lead_copies = at.start(at.to_all_x(lambda to: own, lambda d: own, self.sems[5]))

    def lead_rows(self, k, m):
        rank = self.steps.shape[1]
        pieces = rank // CHUNK
        first = (k - 1) * pieces
        return jnp.concatenate([self.lead[m, first + i].astype(F32) for i in range(pieces)], axis=0)


def lanes_of(m):
    first = (None, 0, LANES, 2 * LANES)[m]
    return slice(first, first + (LANES if m < 3 else 2 * LANES))


def take(refs, count):
    return [refs.pop(0) for _ in range(count)]


def kernel(sides_in, left_in, right_in, known_in, dleft_in, dright_in, inverse_in, updated, solved, *scratch):
    at = Place()
    r, c, go = at.r, at.c, at.go
    refs = list(scratch)
    left, right, known, coeff, sides_raw, sides, dleft_raw, dright_raw, dleft, inverse = take(refs, 10)
    packs, lead_left, base_whole, factors, own_factors, own_left = take(refs, 6)
    wide, lead_coeff = take(refs, 2)
    lead_buffers = take(refs, 4)
    bulk_buffers = [take(refs, 7) for _ in GROUPS[1:]]
    flow_buffers = [take(refs, 8) for _ in range(2)]
    start = flow_buffers[1][0]
    load_sem, gather_send, gather_recv, bulk_send, bulk_recv = take(refs, 5)
    x_send, x_recv, z_send, z_recv = take(refs, 4)
    pack_send, pack_recv, start_send, start_recv = take(refs, 4)
    x_sems = [(x_send.at[i], x_recv.at[i]) for i in range(x_send.shape[0])]
    z_sems = [(z_send.at[i], z_recv.at[i]) for i in range(z_send.shape[0])]

    depth, priors = known_in.shape[1], known_in.shape[0]
    local_rows, steps, thin, rank = dleft_in.shape
    sides_count = sides.shape[2]
    tile = left.shape[3]
    width = steps * rank
    half = packs.shape[2] // 2

    prior = [ReduceDirect(at, lead_buffers, x_sems.pop(), z_sems.pop())]
    for i, buffers in enumerate(bulk_buffers):
        prior.append(Reduce(at, buffers, (bulk_send.at[i], bulk_recv.at[i]), z_sems.pop()))
    lead_all = Gather(at, lead_left, x_sems.pop(), z_sems.pop())
    base_all = Gather(at, base_whole, x_sems.pop(), z_sems.pop(), r < steps)
    flows = [
        Flow(
            at,
            buffers,
            (x_sems.pop(), z_sems.pop(), x_sems.pop(), z_sems.pop(), z_sems.pop(), x_sems.pop()),
            separate,
        )
        for buffers, separate in zip(flow_buffers, (True, False))
    ]
    cross, near = flows
    factor_copies = at.to_all_x(lambda to: factors.at[to], lambda d: own_factors.at[at.x], x_sems.pop())
    left_copies = at.to_all_z(lambda to: dleft.at[to], lambda d: own_left.at[at.z], z_sems.pop())

    loads = [
        pltpu.make_async_copy(src, dst, load_sem.at[i])
        for i, (src, dst) in enumerate(
            (
                (known_in, known.at[:, pl.ds(r * depth, depth)]),
                (dleft_in, dleft_raw),
                (dright_in, dright_raw),
                (right_in, right),
                (left_in, left),
                (inverse_in, inverse),
                (sides_in, sides_raw),
            )
        )
    ]
    for load in loads:
        load.start()
    barrier = pltpu.get_barrier_semaphore()
    peers = [(at.next_r[d], c) for d in range(1, at.rows)]
    peers += [(r, at.along_x[d]) for d in range(1, NX)]
    peers += [(r, at.along_z[d]) for d in range(1, at.nz)]
    for row, col in peers:
        pl.semaphore_signal(barrier, inc=1, device_id={ROW: row, COL: col}, device_id_type=MESH)

    for load in loads[1:3]:
        load.wait()
    factors[...] = jnp.zeros(factors.shape, BF16)
    packs[r] = jnp.zeros(packs.shape[1:], BF16)
    for m in range(steps):
        lanes = slice(m * rank, (m + 1) * rank)
        packs[r, :, lanes] = dleft_raw[0, m]
        packs[r, :, half + m * rank : half + (m + 1) * rank] = dright_raw[0, m]
        for a in range(local_rows):
            dleft[a, :, lanes] = dleft_raw[a, m]
            factors[m, :, a * rank : (a + 1) * rank] = dright_raw[a, m]
    loads[0].wait()
    pl.semaphore_wait(barrier, len(peers))

    def block(row, j):
        return known.at[j, pl.ds(row * depth, depth)]

    def share(row_of_block, j, kind, target):
        part = block(row_of_block, j)
        return remote(part, part, gather_send.at[kind, j], gather_recv.at[kind, j], target, c)

    own_up, own_down, relay, over = [], [], [], [[], [], [], []]
    for j in range(priors):
        own_up.append(go(share(r, j, 0, at.up)))
        own_down.append(go(share(r, j, 1, at.down)))
        over[0].append(go(share(r, j, 3, at.partner)))
    left_copies = at.start(left_copies)
    own_left[at.z] = dleft[at.z]
    for j in range(priors):
        own_up[j].wait_recv()
        over[1].append(go(share(at.down, j, 4, at.partner)))
        if j < priors // 2:
            relay.append(go(share(at.down, j, 2, at.up)))
        own_down[j].wait_recv()
        over[2].append(go(share(at.up, j, 5, at.partner)))
        if j >= priors // 2:
            relay.append(go(share(at.up, j, 2, at.down)))

    sends_pack = jnp.logical_and(r > 0, r < steps)
    pack_copies = [
        remote(packs.at[r], packs.at[r], pack_send.at[d], pack_recv.at[r], at.next_r[d], c)
        for d in range(1, at.rows)
    ]

    @pl.when(sends_pack)
    def _():
        for copy in pack_copies:
            copy.start()

    loads[6].wait()
    whole_sides = sides_raw[...].astype(F32)
    for a in range(local_rows):
        sides[a] = whole_sides[:, a]

    for load in loads[3:6]:
        load.wait()
    for j in range(priors):
        relay[j].wait_recv()
        over[3].append(go(share(at.far, j, 6, at.partner)))
        for kind in range(4):
            over[kind][j].wait_recv()
        product = dot(right[:, j].reshape(-1, tile), known[j])
        coeff[:, pl.ds(j * rank, rank)] = product.astype(BF16).reshape(local_rows, rank, sides_count)

    def multiply(g):
        first = GROUPS[g][0]

        def one(i, carry):
            term = dot(left[i + first].reshape(priors * rank, tile), coeff[i + first], TN)
            term = term.astype(BF16).reshape(at.nz, NX, thin, sides_count)
            for at_x in range(NX):
                prior[g].parts[at_x, :, i] = term[:, at_x]
            return carry

        lax.fori_loop(0, len(GROUPS[g]), one, 0)

    def own_base(g):
        total = prior[g].result()
        for i, a in enumerate(GROUPS[g]):
            updated[a] = sides[a] - total[i]

    multiply(0)
    prior[0].first()

    for k in range(1, steps):

        @pl.when(r != k)
        def _():
            remote(packs.at[k], packs.at[k], pack_send.at[1], pack_recv.at[k], at.next_r[1], c).wait_recv()

    lead_left[at.z, at.x] = jnp.zeros(lead_left.shape[2:], BF16)
    for k in range(1, steps):
        lanes = lanes_of(k)
        lead_left[at.z, at.x, :, lanes.start : lanes.start + k * rank] = packs[k, :, : k * rank]
        for m in range(steps):
            first = (local_rows + k - 1) * rank
            factors[m, :, first : first + rank] = packs[k, :, half + m * rank : half + (m + 1) * rank]
    lead_all.first()
    factor_copies = at.start(factor_copies)
    own_factors[at.x] = factors[at.x]
    multiply(1)
    prior[0].second()
    lead_all.second()
    multiply(2)
    own_base(0)

    @pl.when(r < steps)
    def _():
        base_whole[at.z, at.x] = updated[0].astype(BF16)
        base_all.first()

    lead_all.wait()
    whole_left = lead_left[...].reshape(tile, lead_left.shape[3])
    cross.source[...] = jnp.zeros(cross.source.shape, BF16)
    for m in range(1, steps):
        lanes = lanes_of(m)
        product = dot(inverse[m], whole_left[:, lanes]).astype(BF16)
        wide[:, lanes] = product
        cross.source[m, :, : lanes.stop - lanes.start] = product
    cross.feed()

    @pl.when(r < steps)
    def _():
        base_all.second()

    start_copies = [
        remote(start.at[r], start.at[r], start_send.at[d], start_recv.at[r], at.next_r[d], c)
        for d in range(1, at.rows)
    ]
    landed(factor_copies)
    cross.right(own_factors, local_rows, rank)

    @pl.when(r < steps)
    def _():
        base_all.wait()
        start[r] = dot(inverse[r], base_whole[...].reshape(tile, sides_count)).astype(BF16)
        for copy in start_copies:
            copy.start()

    prior[1].first()
    off = jnp.logical_and(at.z == 0, r <= at.x)
    cross.share(rank, off)
    for k in range(steps):

        @pl.when(r != k)
        def _():
            remote(start.at[k], start.at[k], start_send.at[1], start_recv.at[k], at.next_r[1], c).wait_recv()

    near.feed()
    prior[1].second()
    near.right(own_factors, local_rows, rank)
    prior[2].first()
    landed(left_copies)
    cross.left(own_left)
    cross.lead_x()
    prior[1].third()
    near.share(rank, off)
    prior[2].second()
    near.left(own_left)
    near.lead_x()
    own_base(1)
    prior[2].third()
    landed(cross.lead_copies)
    landed(cross.out_copies)
    landed(near.lead_copies)

    lead_coeff[...] = jnp.zeros(lead_coeff.shape, BF16)
    for m in range(steps - 1):
        for k in range(m + 1, steps):
            value = near.lead_rows(k, m)
            if m:
                lanes = lanes_of(m)
                size = lanes.stop - lanes.start
                value = value - dot(cross.lead_rows(k, m).astype(BF16)[:, :size], lead_coeff[lanes])
            first = lanes_of(k).start + m * rank
            lead_coeff[first : first + rank] = value.astype(BF16)
    for m in range(steps):
        answer = start[m].astype(F32)
        if m:
            answer = answer - dot(wide[:, lanes_of(m)], lead_coeff[lanes_of(m)])
        solved[m] = answer.astype(BF16)
    correction = dot(cross.whole[...].reshape(local_rows * thin, -1), lead_coeff[...])
    correction = correction.reshape(local_rows, thin, sides_count)
    own_base(2)
    landed(near.out_copies)
    for a in range(local_rows):
        updated[a] = updated[a] + (correction[a] - near.whole[a].astype(F32))

    for copy in at.sends:
        copy.close()

    @pl.when(sends_pack)
    def _():
        for copy in pack_copies:
            copy.wait_send()

    @pl.when(r < steps)
    def _():
        for copy in start_copies:
            copy.wait_send()


def local(right_sides, prior_left, prior_right, solved_prior, diag_left, diag_right, diag_inverse):
    thin, local_rows, sides = right_sides.shape
    priors, rank, tile = prior_left.shape[1:]
    diag_left, diag_right = jnp.swapaxes(diag_left, 2, 3), jnp.swapaxes(diag_right, 2, 3)
    steps = diag_left.shape[1]
    rows, cols = lax.axis_size(ROW), lax.axis_size(COL)
    nz = cols // NX
    width = steps * rank
    block = rank + CHUNK
    factor_width = (local_rows + NX - 1) * rank

    shapes = [
        prior_left.shape,
        prior_right.shape,
        (priors, tile, sides),
        (local_rows, priors * rank, sides),
        right_sides.shape,
        ((local_rows, thin, sides), F32),
        diag_left.shape,
        diag_right.shape,
        (local_rows, thin, width),
        diag_inverse.shape,
        (rows, thin, 4 * LANES),
        (nz, NX, thin, 4 * LANES),
        (nz, NX, thin, sides),
        (steps, thin, factor_width),
        (NX, thin, factor_width),
        (nz, thin, width),
        (thin, 4 * LANES),
        (4 * LANES, sides),
    ]
    one = (len(GROUPS[0]), thin, sides)
    shapes += [(NX, nz, *one), (NX - 1, nz, *one), (nz, *one), (nz, *one)]
    for group in GROUPS[1:]:
        for lead in ((NX, nz), (nz // 2,), (nz // 2,), (nz,), (nz,), (nz,), (nz,)):
            shapes.append((*lead, len(group), thin, sides))
    for out in (4 * LANES, sides):
        shapes += [
            (steps, thin, sides),
            (NX, thin, sides),
            (nz, block, sides),
            (nz, block, sides),
            (NX, rank, sides),
            (NX, nz, CHUNK, sides),
            (nz, thin, out),
            (nz, thin, out),
        ]
    scratch = [pltpu.VMEM(*shape) if isinstance(shape[0], tuple) else pltpu.VMEM(shape, BF16) for shape in shapes]
    bulk = len(GROUPS) - 1
    for shape in (
        (7,),
        (7, priors),
        (7, priors),
        (bulk, 6),
        (bulk, 6),
        (10, NX),
        (10, NX),
        (12, nz),
        (12, nz),
        (rows,),
        (steps,),
        (rows,),
        (steps,),
    ):
        scratch.append(pltpu.SemaphoreType.DMA(shape))
    updated, solved = pl.pallas_call(
        kernel,
        out_shape=(
            jax.ShapeDtypeStruct((local_rows, thin, sides), F32),
            jax.ShapeDtypeStruct((steps, thin, sides), BF16),
        ),
        in_specs=[pl.BlockSpec(memory_space=pl.ANY)] * 7,
        out_specs=(pl.BlockSpec(memory_space=pltpu.VMEM), pl.BlockSpec(memory_space=pltpu.VMEM)),
        scratch_shapes=scratch,
        compiler_params=pltpu.CompilerParams(
            collective_id=0, has_side_effects=True, vmem_limit_bytes=56 * 1024 * 1024
        ),
    )(right_sides, prior_left, prior_right, solved_prior, diag_left, diag_right, diag_inverse)
    return jnp.swapaxes(updated, 0, 1), solved


def solution(mesh):
    return jax.shard_map(
        local,
        mesh=mesh,
        in_specs=(
            P(COL, ROW, None),
            P(ROW, COL, None, None),
            P(ROW, COL, None, None),
            P(COL, ROW, None),
            P(ROW, None, None, COL),
            P(ROW, None, None, COL),
            P(None, COL, None),
        ),
        out_specs=(P(COL, ROW, None), P(None, COL, None)),
        check_vma=False,
    )
```

time: 133 us -> 114 us (0.86)
  Pallas kernels: 123 us -> 110 us
  local copies, waits for them, and re-layouts: 8.61 us -> 3.28 us
    pallas_call x1, Pallas kernels: 123 us -> 110 us  [local(): pl.pallas_call(kernel, out_shape=(jax.ShapeDtypeStruct((local_rows, thin,...]
    unnamed x5 -> x2, local copies, waits for them, and re-layouts: 8.61 us -> 3.28 us
where the time goes in v3:
time: 114 us
  Pallas kernels  110 us (96%)
  local copies, waits for them, and re-layouts  3.28 us (3%)
    pallas_call x1, Pallas kernels, local(): pl.pallas_call(kernel, out_shape=(jax.ShapeDtypeStruct((local_rows, thin,...  110 us
    unnamed x2, local copies, waits for them, and re-layouts  3.28 us

profile of v3, /device:TPU:8, one launch (start us, length us, event | category | flops | bytes accessed | tf_op | source)
XLA Modules:
  0.0 113.9 jit_solution(933720339584455826)
XLA Ops:
  0.6 110.0 %shard_map.86 = (f32[8,32,256]{2,1,0:T(8,128)}, bf16[4,32,256]{2,1,0:T(8,128)(2,1)}) custom-call(bf16[32,8,256]{2,1,0:T(8,128)(2,1)} %sides_in.1, bf16[8,4,48,1024]{3,2,1,0:T(8,128)(2,1)} %left_in.1, bf16[8,4,48,1024]{3,2,1,0:T(8,128)(2,1)} %right_in.1, bf16[4,128,256]{2,1,0:T(8,128)(2,1)} %known_in.1, bf16[8,4,32,48]{3,2,1,0:T(8,128)(2,1)} %bitcast.3, ...), custom_call_target="tpu_custom_call" | custom-call | tf_op jit(solution)/shard_map/pallas_call | solution.py:623
  110.6 1.8 %copy.9 = f32[32,8,256]{2,1,0:T(8,128)} copy(f32[32,8,256]{2,0,1:T(8,128)} %bitcast.5) | data formatting | bytes 524288
  112.4 1.5 %copy.11 = bf16[4,32,256]{2,1,0:T(8,128)(2,1)} copy(bf16[4,32,256]{2,1,0:T(8,128)(2,1)} %get-tuple-element.11) | data formatting | bytes 131072

commit v4 on v3

--- a/solution.py
+++ b/solution.py
@@ -13,7 +13,7 @@
 F32 = jnp.float32
 BF16 = jnp.bfloat16
 LANES = 128
-GROUPS = ((0,), (1, 2, 3), (4, 5, 6, 7))
+GROUPS = ((0,), (1, 2), (3, 4), (5, 6, 7))
 CHUNK = 24
 TN = (((0,), (0,)), ((), ()))
 
@@ -293,7 +293,8 @@
     r, c, go = at.r, at.c, at.go
     refs = list(scratch)
     left, right, known, coeff, sides_raw, sides, dleft_raw, dright_raw, dleft, inverse = take(refs, 10)
-    packs, lead_left, base_whole, factors, own_factors, own_left = take(refs, 6)
+    packs, lead_left, factors, own_factors, own_left = take(refs, 5)
+    base_block, columns, start_parts, start_from = take(refs, 4)
     wide, lead_coeff = take(refs, 2)
     lead_buffers = take(refs, 4)
     bulk_buffers = [take(refs, 7) for _ in GROUPS[1:]]
@@ -311,12 +312,29 @@
     tile = left.shape[3]
     width = steps * rank
     half = packs.shape[2] // 2
+    solving = r < steps
+    below = jnp.logical_and(r > 0, solving)
 
     prior = [ReduceDirect(at, lead_buffers, x_sems.pop(), z_sems.pop())]
     for i, buffers in enumerate(bulk_buffers):
         prior.append(Reduce(at, buffers, (bulk_send.at[i], bulk_recv.at[i]), z_sems.pop()))
-    lead_all = Gather(at, lead_left, x_sems.pop(), z_sems.pop())
-    base_all = Gather(at, base_whole, x_sems.pop(), z_sems.pop(), r < steps)
+    lead_all = Gather(at, lead_left, x_sems.pop(), z_sems.pop(), below)
+    base_copies = at.to_all_x(lambda to: base_block.at[at.x], lambda d: base_block.at[at.x], x_sems.pop())
+    start_z_copies = at.to_all_z(lambda to: start_parts.at[to], lambda d: start_from.at[d], z_sems.pop())
+    column_copies = at.to_all_z(
+        lambda to: inverse.at[r % steps, :, pl.ds(pl.multiple_of(to * LANES, LANES), LANES)],
+        lambda d: columns.at[at.z],
+        z_sems.pop(),
+    )
+    start_copies = [
+        remote(start.at[r % steps], start.at[r % steps], start_send.at[d], start_recv.at[r % steps], at.next_r[d], c)
+        for d in range(1, at.rows)
+    ]
+    pack_copies = [
+        remote(packs.at[r], packs.at[r], pack_send.at[d], pack_recv.at[r % steps], at.next_r[d], c)
+        for d in range(1, at.rows)
+    ]
+    running = {}
     flows = [
         Flow(
             at,
@@ -337,9 +355,9 @@
                 (known_in, known.at[:, pl.ds(r * depth, depth)]),
                 (dleft_in, dleft_raw),
                 (dright_in, dright_raw),
+                (inverse_in, inverse),
                 (right_in, right),
                 (left_in, left),
-                (inverse_in, inverse),
                 (sides_in, sides_raw),
             )
         )
@@ -359,11 +377,13 @@
     packs[r] = jnp.zeros(packs.shape[1:], BF16)
     for m in range(steps):
         lanes = slice(m * rank, (m + 1) * rank)
-        packs[r, :, lanes] = dleft_raw[0, m]
         packs[r, :, half + m * rank : half + (m + 1) * rank] = dright_raw[0, m]
         for a in range(local_rows):
             dleft[a, :, lanes] = dleft_raw[a, m]
             factors[m, :, a * rank : (a + 1) * rank] = dright_raw[a, m]
+    lead_left[at.z, at.x] = jnp.zeros(lead_left.shape[2:], BF16)
+    for m in range(steps - 1):
+        lead_left[at.z, at.x, :, m * rank : (m + 1) * rank] = dleft_raw[0, m]
     loads[0].wait()
     pl.semaphore_wait(barrier, len(peers))
 
@@ -379,6 +399,17 @@
         own_up.append(go(share(r, j, 0, at.up)))
         own_down.append(go(share(r, j, 1, at.down)))
         over[0].append(go(share(r, j, 3, at.partner)))
+    @pl.when(below)
+    def _():
+        lead_all.first()
+
+    loads[3].wait()
+
+    @pl.when(solving)
+    def _():
+        running["columns"] = at.start(column_copies, solving)
+        columns[at.z] = inverse[r % steps, :, pl.ds(pl.multiple_of(at.z * LANES, LANES), LANES)]
+
     left_copies = at.start(left_copies)
     own_left[at.z] = dleft[at.z]
     for j in range(priors):
@@ -391,23 +422,16 @@
         if j >= priors // 2:
             relay.append(go(share(at.up, j, 2, at.down)))
 
-    sends_pack = jnp.logical_and(r > 0, r < steps)
-    pack_copies = [
-        remote(packs.at[r], packs.at[r], pack_send.at[d], pack_recv.at[r], at.next_r[d], c)
-        for d in range(1, at.rows)
-    ]
-
-    @pl.when(sends_pack)
-    def _():
-        for copy in pack_copies:
-            copy.start()
+    @pl.when(below)
+    def _():
+        lead_all.second()
 
     loads[6].wait()
     whole_sides = sides_raw[...].astype(F32)
     for a in range(local_rows):
         sides[a] = whole_sides[:, a]
 
-    for load in loads[3:6]:
+    for load in loads[4:6]:
         load.wait()
     for j in range(priors):
         relay[j].wait_recv()
@@ -437,64 +461,70 @@
     multiply(0)
     prior[0].first()
 
+    @pl.when(below)
+    def _():
+        lead_all.wait()
+        product = dot(inverse[r % steps], lead_left[...].reshape(tile, half))
+        lane = lax.broadcasted_iota(jnp.int32, product.shape, 1)
+        packs[r, :, :half] = jnp.where(lane < r * rank, product, 0.0).astype(BF16)
+        for copy in pack_copies:
+            copy.start()
+
+    multiply(1)
+    multiply(2)
+    prior[0].second()
+    prior[1].first()
     for k in range(1, steps):
 
         @pl.when(r != k)
         def _():
             remote(packs.at[k], packs.at[k], pack_send.at[1], pack_recv.at[k], at.next_r[1], c).wait_recv()
 
-    lead_left[at.z, at.x] = jnp.zeros(lead_left.shape[2:], BF16)
+    cross.source[0] = jnp.zeros(cross.source.shape[1:], BF16)
     for k in range(1, steps):
         lanes = lanes_of(k)
-        lead_left[at.z, at.x, :, lanes.start : lanes.start + k * rank] = packs[k, :, : k * rank]
+        wide[:, lanes] = packs[k, :, : lanes.stop - lanes.start]
+        cross.source[k] = packs[k, :, :half]
         for m in range(steps):
             first = (local_rows + k - 1) * rank
             factors[m, :, first : first + rank] = packs[k, :, half + m * rank : half + (m + 1) * rank]
-    lead_all.first()
+    cross.feed()
     factor_copies = at.start(factor_copies)
     own_factors[at.x] = factors[at.x]
-    multiply(1)
-    prior[0].second()
-    lead_all.second()
-    multiply(2)
     own_base(0)
 
-    @pl.when(r < steps)
-    def _():
-        base_whole[at.z, at.x] = updated[0].astype(BF16)
-        base_all.first()
-
-    lead_all.wait()
-    whole_left = lead_left[...].reshape(tile, lead_left.shape[3])
-    cross.source[...] = jnp.zeros(cross.source.shape, BF16)
-    for m in range(1, steps):
-        lanes = lanes_of(m)
-        product = dot(inverse[m], whole_left[:, lanes]).astype(BF16)
-        wide[:, lanes] = product
-        cross.source[m, :, : lanes.stop - lanes.start] = product
-    cross.feed()
-
-    @pl.when(r < steps)
-    def _():
-        base_all.second()
-
-    start_copies = [
-        remote(start.at[r], start.at[r], start_send.at[d], start_recv.at[r], at.next_r[d], c)
-        for d in range(1, at.rows)
-    ]
+    @pl.when(solving)
+    def _():
+        base_block[at.x] = updated[0].astype(BF16)
+        running["base"] = at.start(base_copies, solving)
+
+    multiply(3)
+
+    @pl.when(solving)
+    def _():
+        landed(running["columns"])
+        landed(running["base"])
+        product = dot(columns[...].reshape(-1, LANES), base_block[...].reshape(-1, sides_count))
+        start_parts[...] = product.astype(BF16).reshape(start_parts.shape)
+        running["start"] = at.start(start_z_copies, solving)
+
+    prior[1].second()
+    prior[2].first()
     landed(factor_copies)
     cross.right(own_factors, local_rows, rank)
 
-    @pl.when(r < steps)
-    def _():
-        base_all.wait()
-        start[r] = dot(inverse[r], base_whole[...].reshape(tile, sides_count)).astype(BF16)
+    @pl.when(solving)
+    def _():
+        landed(running["start"])
+        total = start_parts[at.z].astype(F32)
+        for d in range(1, at.nz):
+            total = total + start_from[d].astype(F32)
+        start[r % steps] = total.astype(BF16)
         for copy in start_copies:
             copy.start()
 
-    prior[1].first()
+    prior[1].third()
     off = jnp.logical_and(at.z == 0, r <= at.x)
-    cross.share(rank, off)
     for k in range(steps):
 
         @pl.when(r != k)
@@ -502,19 +532,21 @@
             remote(start.at[k], start.at[k], start_send.at[1], start_recv.at[k], at.next_r[1], c).wait_recv()
 
     near.feed()
-    prior[1].second()
+    prior[2].second()
+    prior[3].first()
     near.right(own_factors, local_rows, rank)
-    prior[2].first()
+    cross.share(rank, off)
     landed(left_copies)
+    prior[2].third()
     cross.left(own_left)
+    near.share(rank, off)
+    prior[3].second()
     cross.lead_x()
-    prior[1].third()
-    near.share(rank, off)
-    prior[2].second()
     near.left(own_left)
+    prior[3].third()
     near.lead_x()
     own_base(1)
-    prior[2].third()
+    own_base(2)
     landed(cross.lead_copies)
     landed(cross.out_copies)
     landed(near.lead_copies)
@@ -536,7 +568,7 @@
         solved[m] = answer.astype(BF16)
     correction = dot(cross.whole[...].reshape(local_rows * thin, -1), lead_coeff[...])
     correction = correction.reshape(local_rows, thin, sides_count)
-    own_base(2)
+    own_base(3)
     landed(near.out_copies)
     for a in range(local_rows):
         updated[a] = updated[a] + (correction[a] - near.whole[a].astype(F32))
@@ -544,15 +576,21 @@
     for copy in at.sends:
         copy.close()
 
-    @pl.when(sends_pack)
+    @pl.when(below)
     def _():
         for copy in pack_copies:
             copy.wait_send()
 
-    @pl.when(r < steps)
+    @pl.when(solving)
     def _():
         for copy in start_copies:
             copy.wait_send()
+
+
+def place_results(updated, solved, updated_out, solved_out):
+    for a in range(updated.shape[0]):
+        updated_out[:, a] = updated[a]
+    solved_out[...] = solved[...]
 
 
 def local(right_sides, prior_left, prior_right, solved_prior, diag_left, diag_right, diag_inverse):
@@ -578,11 +616,14 @@
         (local_rows, thin, width),
         diag_inverse.shape,
         (rows, thin, 4 * LANES),
-        (nz, NX, thin, 4 * LANES),
-        (nz, NX, thin, sides),
+        (nz, NX, thin, 2 * LANES),
         (steps, thin, factor_width),
         (NX, thin, factor_width),
         (nz, thin, width),
+        (NX, thin, sides),
+        (nz, thin, LANES),
+        (nz, thin, sides),
+        (nz, thin, sides),
         (thin, 4 * LANES),
         (4 * LANES, sides),
     ]
@@ -612,8 +653,8 @@
         (bulk, 6),
         (10, NX),
         (10, NX),
-        (12, nz),
-        (12, nz),
+        (14, nz),
+        (14, nz),
         (rows,),
         (steps,),
         (rows,),
@@ -633,7 +674,13 @@
             collective_id=0, has_side_effects=True, vmem_limit_bytes=56 * 1024 * 1024
         ),
     )(right_sides, prior_left, prior_right, solved_prior, diag_left, diag_right, diag_inverse)
-    return jnp.swapaxes(updated, 0, 1), solved
+    return pl.pallas_call(
+        place_results,
+        out_shape=(
+            jax.ShapeDtypeStruct((thin, local_rows, sides), F32),
+            jax.ShapeDtypeStruct(solved.shape, BF16),
+        ),
+    )(updated, solved)
 
 
 def solution(mesh):

time: 114 us -> 101 us (0.89); the launches traced: 114 us -> 99.2 us
  Pallas kernels: 110 us -> 98.5 us
  local copies, waits for them, and re-layouts: 3.28 us -> 0 us
    pallas_call x1, Pallas kernels: 110 us -> 96.8 us  [local(): pl.pallas_call(kernel, out_shape=(jax.ShapeDtypeStruct((local_rows, thin,...]
    unnamed x2 -> x0, local copies, waits for them, and re-layouts: 3.28 us -> none
    pallas_call x0 -> x1, Pallas kernels: none -> 1.75 us  [local(): pl.pallas_call(place_results, out_shape=(jax.ShapeDtypeStruct((thin, loca...]
where the time goes in v4:
time: 101 us; the launch traced here: 99.2 us
  Pallas kernels  98.5 us (98%)
    pallas_call x1, Pallas kernels, local(): pl.pallas_call(kernel, out_shape=(jax.ShapeDtypeStruct((local_rows, thin,...  96.8 us

profile of v4, /device:TPU:8, one launch (start us, length us, event | category | flops | bytes accessed | tf_op | source)
XLA Modules:
  0.0 99.2 jit_solution(16649493602632841375)
XLA Ops:
  0.6 96.8 %shard_map.86 = (f32[8,32,256]{2,1,0:T(8,128)}, bf16[4,32,256]{2,1,0:T(8,128)(2,1)}) custom-call(bf16[32,8,256]{2,1,0:T(8,128)(2,1)} %sides_in.1, bf16[8,4,48,1024]{3,2,1,0:T(8,128)(2,1)} %left_in.1, bf16[8,4,48,1024]{3,2,1,0:T(8,128)(2,1)} %right_in.1, bf16[4,128,256]{2,1,0:T(8,128)(2,1)} %known_in.1, bf16[8,4,32,48]{3,2,1,0:T(8,128)(2,1)} %bitcast.2, ...), custom_call_target="tpu_custom_call" | custom-call | tf_op jit(solution)/shard_map/pallas_call | solution.py:664
  97.4 1.7 %shard_map.87 = (f32[32,8,256]{2,1,0:T(8,128)}, bf16[4,32,256]{2,1,0:T(8,128)(2,1)}) custom-call(f32[8,32,256]{2,1,0:T(8,128)} %get-tuple-element.4.updated, bf16[4,32,256]{2,1,0:T(8,128)(2,1)} %get-tuple-element.5.solved), custom_call_target="tpu_custom_call" | custom-call | tf_op jit(solution)/shard_map/pallas_call | solution.py:677

commit v5 on v4

--- a/solution.py
+++ b/solution.py
@@ -15,6 +15,7 @@
 LANES = 128
 GROUPS = ((0,), (1, 2), (3, 4), (5, 6, 7))
 CHUNK = 24
+LEAD_X_AT = 3
 TN = (((0,), (0,)), ((), ()))
 
 
@@ -208,7 +209,8 @@
 class Flow:
     def __init__(self, at, buffers, sems, separate):
         self.at, self.separate = at, separate
-        self.source, self.block, self.parts, self.from_z, self.steps, self.lead, self.out, self.whole = buffers
+        self.source, self.block, self.parts, self.from_z, self.steps, self.lead, self.out, self.whole = buffers[:8]
+        self.lead_parts, self.lead_from_z = buffers[8:]
         self.sems = sems
 
     def feed(self):
@@ -223,29 +225,39 @@
         landed(self.fed)
         count, thin, sides = self.block.shape
         product = dot(factors[...].reshape(count * thin, -1), self.block[...].reshape(count * thin, sides), TN)
-        self.parts[:, :rank] = product[: positions * rank].astype(BF16).reshape(positions, rank, sides)
+        self.parts[...] = product[: positions * rank].astype(BF16).reshape(positions, rank, sides)
+        self.z_copies = at.start(
+            at.to_all_z(lambda to: self.parts.at[to], lambda d: self.from_z.at[d], self.sems[1])
+        )
         lead = product[positions * rank :]
         chunks = (NX - 1) * rank // CHUNK
         for i in range(at.nz):
             part = lead[i * CHUNK : (i + 1) * CHUNK] if i < chunks else jnp.zeros((CHUNK, sides), F32)
-            self.parts[i, rank:] = part.astype(BF16)
-        self.z_copies = at.start(
-            at.to_all_z(lambda to: self.parts.at[to], lambda d: self.from_z.at[d], self.sems[1])
-        )
-
-    def share(self, rank, off):
+            self.lead_parts[i] = part.astype(BF16)
+        self.lead_sums = at.start(
+            at.to_all_z(lambda to: self.lead_parts.at[to], lambda d: self.lead_from_z.at[d], self.sems[6])
+        )
+
+    def share(self, off):
         at = self.at
         landed(self.z_copies)
         total = self.parts[at.z].astype(F32)
         for d in range(1, at.nz):
             total = total + self.from_z[d].astype(F32)
-        self.steps[at.x] = jnp.where(off, 0.0, total[:rank]).astype(BF16)
-        self.lead[at.x, at.z] = total[rank:].astype(BF16)
+        self.steps[at.x] = jnp.where(off, 0.0, total).astype(BF16)
         self.x_copies = at.start(
             at.to_all_x(lambda to: self.steps.at[at.x], lambda d: self.steps.at[at.x], self.sems[2])
         )
+
+    def lead_z(self):
+        at = self.at
+        landed(self.lead_sums)
+        total = self.lead_parts[at.z].astype(F32)
+        for d in range(1, at.nz):
+            total = total + self.lead_from_z[d].astype(F32)
+        self.lead[at.x, at.z] = total.astype(BF16)
         own = self.lead.at[at.x, at.z]
-        self.lead_z = at.start(at.to_all_z(lambda to: own, lambda d: own, self.sems[3]))
+        self.lead_all = at.start(at.to_all_z(lambda to: own, lambda d: own, self.sems[3]))
 
     def left(self, factors):
         at = self.at
@@ -268,7 +280,7 @@
 
     def lead_x(self):
         at = self.at
-        landed(self.lead_z)
+        landed(self.lead_all)
         own = self.lead.at[at.x]
         self.lead_copies = at.start(at.to_all_x(lambda to: own, lambda d: own, self.sems[5]))
 
@@ -298,7 +310,7 @@
     wide, lead_coeff = take(refs, 2)
     lead_buffers = take(refs, 4)
     bulk_buffers = [take(refs, 7) for _ in GROUPS[1:]]
-    flow_buffers = [take(refs, 8) for _ in range(2)]
+    flow_buffers = [take(refs, 10) for _ in range(2)]
     start = flow_buffers[1][0]
     load_sem, gather_send, gather_recv, bulk_send, bulk_recv = take(refs, 5)
     x_send, x_recv, z_send, z_recv = take(refs, 4)
@@ -339,7 +351,7 @@
         Flow(
             at,
             buffers,
-            (x_sems.pop(), z_sems.pop(), x_sems.pop(), z_sems.pop(), z_sems.pop(), x_sems.pop()),
+            (x_sems.pop(), z_sems.pop(), x_sems.pop(), z_sems.pop(), z_sems.pop(), x_sems.pop(), z_sems.pop()),
             separate,
         )
         for buffers, separate in zip(flow_buffers, (True, False))
@@ -371,6 +383,21 @@
     for row, col in peers:
         pl.semaphore_signal(barrier, inc=1, device_id={ROW: row, COL: col}, device_id_type=MESH)
 
+    loads[0].wait()
+    pl.semaphore_wait(barrier, len(peers))
+
+    def block(row, j):
+        return known.at[j, pl.ds(row * depth, depth)]
+
+    def share(row_of_block, j, kind, target):
+        part = block(row_of_block, j)
+        return remote(part, part, gather_send.at[kind, j], gather_recv.at[kind, j], target, c)
+
+    own_up, own_down, relay, over = [], [], [], [[], [], [], []]
+    for j in range(priors):
+        own_up.append(go(share(r, j, 0, at.up)))
+        own_down.append(go(share(r, j, 1, at.down)))
+        over[0].append(go(share(r, j, 3, at.partner)))
     for load in loads[1:3]:
         load.wait()
     factors[...] = jnp.zeros(factors.shape, BF16)
@@ -384,21 +411,7 @@
     lead_left[at.z, at.x] = jnp.zeros(lead_left.shape[2:], BF16)
     for m in range(steps - 1):
         lead_left[at.z, at.x, :, m * rank : (m + 1) * rank] = dleft_raw[0, m]
-    loads[0].wait()
-    pl.semaphore_wait(barrier, len(peers))
-
-    def block(row, j):
-        return known.at[j, pl.ds(row * depth, depth)]
-
-    def share(row_of_block, j, kind, target):
-        part = block(row_of_block, j)
-        return remote(part, part, gather_send.at[kind, j], gather_recv.at[kind, j], target, c)
-
-    own_up, own_down, relay, over = [], [], [], [[], [], [], []]
-    for j in range(priors):
-        own_up.append(go(share(r, j, 0, at.up)))
-        own_down.append(go(share(r, j, 1, at.down)))
-        over[0].append(go(share(r, j, 3, at.partner)))
+
     @pl.when(below)
     def _():
         lead_all.first()
@@ -421,10 +434,11 @@
         over[2].append(go(share(at.up, j, 5, at.partner)))
         if j >= priors // 2:
             relay.append(go(share(at.up, j, 2, at.down)))
-
-    @pl.when(below)
-    def _():
-        lead_all.second()
+        if j == LEAD_X_AT:
+
+            @pl.when(below)
+            def _():
+                lead_all.second()
 
     loads[6].wait()
     whole_sides = sides_raw[...].astype(F32)
@@ -460,7 +474,6 @@
 
     multiply(0)
     prior[0].first()
-
     @pl.when(below)
     def _():
         lead_all.wait()
@@ -473,7 +486,6 @@
     multiply(1)
     multiply(2)
     prior[0].second()
-    prior[1].first()
     for k in range(1, steps):
 
         @pl.when(r != k)
@@ -491,15 +503,16 @@
     cross.feed()
     factor_copies = at.start(factor_copies)
     own_factors[at.x] = factors[at.x]
+    prior[1].first()
     own_base(0)
-
     @pl.when(solving)
     def _():
         base_block[at.x] = updated[0].astype(BF16)
         running["base"] = at.start(base_copies, solving)
 
+    landed(factor_copies)
+    cross.right(own_factors, local_rows, rank)
     multiply(3)
-
     @pl.when(solving)
     def _():
         landed(running["columns"])
@@ -510,9 +523,7 @@
 
     prior[1].second()
     prior[2].first()
-    landed(factor_copies)
-    cross.right(own_factors, local_rows, rank)
-
+    off = jnp.logical_and(at.z == 0, r <= at.x)
     @pl.when(solving)
     def _():
         landed(running["start"])
@@ -524,7 +535,8 @@
             copy.start()
 
     prior[1].third()
-    off = jnp.logical_and(at.z == 0, r <= at.x)
+    cross.share(off)
+    cross.lead_z()
     for k in range(steps):
 
         @pl.when(r != k)
@@ -535,13 +547,13 @@
     prior[2].second()
     prior[3].first()
     near.right(own_factors, local_rows, rank)
-    cross.share(rank, off)
     landed(left_copies)
+    cross.left(own_left)
+    cross.lead_x()
     prior[2].third()
-    cross.left(own_left)
-    near.share(rank, off)
+    near.share(off)
+    near.lead_z()
     prior[3].second()
-    cross.lead_x()
     near.left(own_left)
     prior[3].third()
     near.lead_x()
@@ -601,7 +613,6 @@
     rows, cols = lax.axis_size(ROW), lax.axis_size(COL)
     nz = cols // NX
     width = steps * rank
-    block = rank + CHUNK
     factor_width = (local_rows + NX - 1) * rank
 
     shapes = [
@@ -636,12 +647,14 @@
         shapes += [
             (steps, thin, sides),
             (NX, thin, sides),
-            (nz, block, sides),
-            (nz, block, sides),
+            (nz, rank, sides),
+            (nz, rank, sides),
             (NX, rank, sides),
             (NX, nz, CHUNK, sides),
             (nz, thin, out),
             (nz, thin, out),
+            (nz, CHUNK, sides),
+            (nz, CHUNK, sides),
         ]
     scratch = [pltpu.VMEM(*shape) if isinstance(shape[0], tuple) else pltpu.VMEM(shape, BF16) for shape in shapes]
     bulk = len(GROUPS) - 1
@@ -653,8 +666,8 @@
         (bulk, 6),
         (10, NX),
         (10, NX),
-        (14, nz),
-        (14, nz),
+        (17, nz),
+        (17, nz),
         (rows,),
         (steps,),
         (rows,),

time: 101 us -> 97.3 us (0.963); the launches traced: 99.2 us -> 96.9 us
  Pallas kernels: 98.5 us -> 96.3 us
    pallas_call x1, Pallas kernels: 96.8 us -> 94.5 us  [local(): pl.pallas_call(kernel, out_shape=(jax.ShapeDtypeStruct((local_rows, thin,...]
where the time goes in v5:
time: 97.3 us; the launch traced here: 96.9 us
  Pallas kernels  96.3 us (99%)
    pallas_call x1, Pallas kernels, local(): pl.pallas_call(kernel, out_shape=(jax.ShapeDtypeStruct((local_rows, thin,...  94.5 us

profile of v5, /device:TPU:8, one launch (start us, length us, event | category | flops | bytes accessed | tf_op | source)
XLA Modules:
  0.0 96.9 jit_solution(15041190211144418235)
XLA Ops:
  0.6 94.5 %shard_map.86 = (f32[8,32,256]{2,1,0:T(8,128)}, bf16[4,32,256]{2,1,0:T(8,128)(2,1)}) custom-call(bf16[32,8,256]{2,1,0:T(8,128)(2,1)} %sides_in.1, bf16[8,4,48,1024]{3,2,1,0:T(8,128)(2,1)} %left_in.1, bf16[8,4,48,1024]{3,2,1,0:T(8,128)(2,1)} %right_in.1, bf16[4,128,256]{2,1,0:T(8,128)(2,1)} %known_in.1, bf16[8,4,32,48]{3,2,1,0:T(8,128)(2,1)} %bitcast.2, ...), custom_call_target="tpu_custom_call" | custom-call | tf_op jit(solution)/shard_map/pallas_call | solution.py:677
  95.2 1.7 %shard_map.87 = (f32[32,8,256]{2,1,0:T(8,128)}, bf16[4,32,256]{2,1,0:T(8,128)(2,1)}) custom-call(f32[8,32,256]{2,1,0:T(8,128)} %get-tuple-element.4.updated, bf16[4,32,256]{2,1,0:T(8,128)(2,1)} %get-tuple-element.5.solved), custom_call_target="tpu_custom_call" | custom-call | tf_op jit(solution)/shard_map/pallas_call | solution.py:690

commit v6 on v5

--- a/solution.py
+++ b/solution.py
@@ -233,7 +233,7 @@
         chunks = (NX - 1) * rank // CHUNK
         for i in range(at.nz):
             part = lead[i * CHUNK : (i + 1) * CHUNK] if i < chunks else jnp.zeros((CHUNK, sides), F32)
-            self.lead_parts[i] = part.astype(BF16)
+            self.lead_parts[i] = part[:, : self.lead_parts.shape[2]].astype(BF16)
         self.lead_sums = at.start(
             at.to_all_z(lambda to: self.lead_parts.at[to], lambda d: self.lead_from_z.at[d], self.sems[6])
         )
@@ -269,7 +269,9 @@
             for m in range(1, NX):
                 lanes = lanes_of(m)
                 product = dot(rows[:, m * rank : (m + 1) * rank], self.steps[m, :, : lanes.stop - lanes.start])
-                self.out[:, :, lanes] = product.astype(BF16).reshape(nz, thin, -1)
+                first = m * (m - 1) // 2 * rank
+                product = product[:, : m * rank].astype(BF16).reshape(nz, thin, m * rank)
+                self.out[:, :, first : first + m * rank] = product
         else:
             product = dot(rows, self.steps[...].reshape(width, -1))
             self.out[...] = product.astype(BF16).reshape(nz, thin, -1)
@@ -281,7 +283,7 @@
     def lead_x(self):
         at = self.at
         landed(self.lead_all)
-        own = self.lead.at[at.x]
+        own = self.lead.at[at.x, pl.ds(0, (NX - 1) * self.steps.shape[1] // CHUNK)]
         self.lead_copies = at.start(at.to_all_x(lambda to: own, lambda d: own, self.sems[5]))
 
     def lead_rows(self, k, m):
@@ -307,7 +309,7 @@
     left, right, known, coeff, sides_raw, sides, dleft_raw, dright_raw, dleft, inverse = take(refs, 10)
     packs, lead_left, factors, own_factors, own_left = take(refs, 5)
     base_block, columns, start_parts, start_from = take(refs, 4)
-    wide, lead_coeff = take(refs, 2)
+    wide, lead_coeff, joined = take(refs, 3)
     lead_buffers = take(refs, 4)
     bulk_buffers = [take(refs, 7) for _ in GROUPS[1:]]
     flow_buffers = [take(refs, 10) for _ in range(2)]
@@ -483,9 +485,6 @@
         for copy in pack_copies:
             copy.start()
 
-    multiply(1)
-    multiply(2)
-    prior[0].second()
     for k in range(1, steps):
 
         @pl.when(r != k)
@@ -493,6 +492,7 @@
             remote(packs.at[k], packs.at[k], pack_send.at[1], pack_recv.at[k], at.next_r[1], c).wait_recv()
 
     cross.source[0] = jnp.zeros(cross.source.shape[1:], BF16)
+    cross.out[...] = jnp.zeros(cross.out.shape, BF16)
     for k in range(1, steps):
         lanes = lanes_of(k)
         wide[:, lanes] = packs[k, :, : lanes.stop - lanes.start]
@@ -503,6 +503,9 @@
     cross.feed()
     factor_copies = at.start(factor_copies)
     own_factors[at.x] = factors[at.x]
+    multiply(1)
+    multiply(2)
+    prior[0].second()
     prior[1].first()
     own_base(0)
     @pl.when(solving)
@@ -549,14 +552,14 @@
     near.right(own_factors, local_rows, rank)
     landed(left_copies)
     cross.left(own_left)
-    cross.lead_x()
     prior[2].third()
     near.share(off)
     near.lead_z()
     prior[3].second()
     near.left(own_left)
+    near.lead_x()
+    cross.lead_x()
     prior[3].third()
-    near.lead_x()
     own_base(1)
     own_base(2)
     landed(cross.lead_copies)
@@ -578,7 +581,11 @@
         if m:
             answer = answer - dot(wide[:, lanes_of(m)], lead_coeff[lanes_of(m)])
         solved[m] = answer.astype(BF16)
-    correction = dot(cross.whole[...].reshape(local_rows * thin, -1), lead_coeff[...])
+    joined[...] = jnp.zeros(joined.shape, BF16)
+    for m in range(1, steps):
+        first = m * (m - 1) // 2 * rank
+        joined[first : first + m * rank] = lead_coeff[lanes_of(m).start : lanes_of(m).start + m * rank]
+    correction = dot(cross.whole[...].reshape(local_rows * thin, -1), joined[...])
     correction = correction.reshape(local_rows, thin, sides_count)
     own_base(3)
     landed(near.out_copies)
@@ -637,24 +644,25 @@
         (nz, thin, sides),
         (thin, 4 * LANES),
         (4 * LANES, sides),
+        (3 * LANES, sides),
     ]
     one = (len(GROUPS[0]), thin, sides)
     shapes += [(NX, nz, *one), (NX - 1, nz, *one), (nz, *one), (nz, *one)]
     for group in GROUPS[1:]:
         for lead in ((NX, nz), (nz // 2,), (nz // 2,), (nz,), (nz,), (nz,), (nz,)):
             shapes.append((*lead, len(group), thin, sides))
-    for out in (4 * LANES, sides):
+    for out, lead_lanes in ((3 * LANES, LANES), (sides, sides)):
         shapes += [
             (steps, thin, sides),
             (NX, thin, sides),
             (nz, rank, sides),
             (nz, rank, sides),
             (NX, rank, sides),
-            (NX, nz, CHUNK, sides),
+            (NX, nz, CHUNK, lead_lanes),
             (nz, thin, out),
             (nz, thin, out),
-            (nz, CHUNK, sides),
-            (nz, CHUNK, sides),
+            (nz, CHUNK, lead_lanes),
+            (nz, CHUNK, lead_lanes),
         ]
     scratch = [pltpu.VMEM(*shape) if isinstance(shape[0], tuple) else pltpu.VMEM(shape, BF16) for shape in shapes]
     bulk = len(GROUPS) - 1

time: 97.3 us -> 95.1 us (0.977)
  Pallas kernels: 96.3 us -> 94.2 us
    pallas_call x1, Pallas kernels: 94.5 us -> 92.5 us  [local(): pl.pallas_call(kernel, out_shape=(jax.ShapeDtypeStruct((local_rows, thin,...]
where the time goes in v6:
time: 95.1 us; the launch traced here: 94.9 us
  Pallas kernels  94.2 us (99%)
    pallas_call x1, Pallas kernels, local(): pl.pallas_call(kernel, out_shape=(jax.ShapeDtypeStruct((local_rows, thin,...  92.5 us

profile of v6, /device:TPU:8, one launch (start us, length us, event | category | flops | bytes accessed | tf_op | source)
XLA Modules:
  0.0 94.9 jit_solution(12361665298295161489)
XLA Ops:
  0.6 92.5 %shard_map.86 = (f32[8,32,256]{2,1,0:T(8,128)}, bf16[4,32,256]{2,1,0:T(8,128)(2,1)}) custom-call(bf16[32,8,256]{2,1,0:T(8,128)(2,1)} %sides_in.1, bf16[8,4,48,1024]{3,2,1,0:T(8,128)(2,1)} %left_in.1, bf16[8,4,48,1024]{3,2,1,0:T(8,128)(2,1)} %right_in.1, bf16[4,128,256]{2,1,0:T(8,128)(2,1)} %known_in.1, bf16[8,4,32,48]{3,2,1,0:T(8,128)(2,1)} %bitcast.2, ...), custom_call_target="tpu_custom_call" | custom-call | tf_op jit(solution)/shard_map/pallas_call | solution.py:685
  93.1 1.7 %shard_map.87 = (f32[32,8,256]{2,1,0:T(8,128)}, bf16[4,32,256]{2,1,0:T(8,128)(2,1)}) custom-call(f32[8,32,256]{2,1,0:T(8,128)} %get-tuple-element.4.updated, bf16[4,32,256]{2,1,0:T(8,128)(2,1)} %get-tuple-element.5.solved), custom_call_target="tpu_custom_call" | custom-call | tf_op jit(solution)/shard_map/pallas_call | solution.py:698

commit v7 on v6

--- a/solution.py
+++ b/solution.py
@@ -539,6 +539,8 @@
 
     prior[1].third()
     cross.share(off)
+    landed(left_copies)
+    cross.left(own_left)
     cross.lead_z()
     for k in range(steps):
 
@@ -550,8 +552,6 @@
     prior[2].second()
     prior[3].first()
     near.right(own_factors, local_rows, rank)
-    landed(left_copies)
-    cross.left(own_left)
     prior[2].third()
     near.share(off)
     near.lead_z()

time: 95.1 us -> 93.5 us (0.983)
  Pallas kernels: 94.2 us -> 91.7 us
    pallas_call x1, Pallas kernels: 92.5 us -> 90 us  [local(): pl.pallas_call(kernel, out_shape=(jax.ShapeDtypeStruct((local_rows, thin,...]
where the time goes in v7:
time: 93.5 us; the launch traced here: 92.4 us
  Pallas kernels  91.7 us (98%)
    pallas_call x1, Pallas kernels, local(): pl.pallas_call(kernel, out_shape=(jax.ShapeDtypeStruct((local_rows, thin,...  90 us

profile of v7, /device:TPU:8, one launch (start us, length us, event | category | flops | bytes accessed | tf_op | source)
XLA Modules:
  0.0 92.4 jit_solution(11114767558166219945)
XLA Ops:
  0.6 90.0 %shard_map.86 = (f32[8,32,256]{2,1,0:T(8,128)}, bf16[4,32,256]{2,1,0:T(8,128)(2,1)}) custom-call(bf16[32,8,256]{2,1,0:T(8,128)(2,1)} %sides_in.1, bf16[8,4,48,1024]{3,2,1,0:T(8,128)(2,1)} %left_in.1, bf16[8,4,48,1024]{3,2,1,0:T(8,128)(2,1)} %right_in.1, bf16[4,128,256]{2,1,0:T(8,128)(2,1)} %known_in.1, bf16[8,4,32,48]{3,2,1,0:T(8,128)(2,1)} %bitcast.2, ...), custom_call_target="tpu_custom_call" | custom-call | tf_op jit(solution)/shard_map/pallas_call | solution.py:685
  90.6 1.7 %shard_map.87 = (f32[32,8,256]{2,1,0:T(8,128)}, bf16[4,32,256]{2,1,0:T(8,128)(2,1)}) custom-call(f32[8,32,256]{2,1,0:T(8,128)} %get-tuple-element.4.updated, bf16[4,32,256]{2,1,0:T(8,128)(2,1)} %get-tuple-element.5.solved), custom_call_target="tpu_custom_call" | custom-call | tf_op jit(solution)/shard_map/pallas_call | solution.py:698
